TPU v7x, 32 devices: a whole 2x2x4 slice. The times are simulated.
32 devices in a mesh: groups: 2 (over x), ta: 16 (over z, y, core).
Axes of the slice: x: 2, y: 2, z: 4, core: 2. Of those that a mesh axis runs over, the one named last changes fastest.
Arguments:
- source: float32 [32, 4, 32, 256], P(('groups', 'ta')), parts along dimension 0, may hold values from -13 to 13
- links: float32 [16, 4, 9, 256, 256], P('ta'), may hold values from -0.046875 to 0.046875
- prolongator: float32 [16, 4, 16, 256], P('ta'), may hold values from -0.375 to 0.375
- coarse_inverse: float32 [1024, 1024], P('ta'), may hold values from -1 to 2
Outputs:
- solution: float32 [32, 4, 32, 256], P(('groups', 'ta')), parts along dimension 0
- residual: float32 [32, 4, 32, 256], P(('groups', 'ta')), parts along dimension 0
There are 2 independent parts, one for each index of `groups`. A program takes and returns all parts, laid end to end along the dimension named above; an argument that names none is the same for every part. Nothing has to cross between parts.
All inputs are finite; a program needn't handle non-finite values.
Results may differ from a plain program's by a relative error of at most 0.0003.
Values sent between devices are 32-bit elements; how exact they have to be, the bound alone decides.
A program may use at most 64 MiB of HBM per device.

v0:
```python
import functools

import jax
import jax.numpy as jnp
from jax import lax
from jax.experimental import pallas as pl
from jax.experimental.pallas import tpu as pltpu
from jax.sharding import PartitionSpec as P

LINK_SUMS = ((0, 3, 4), (5, 6), (7, 8), (1,), (2,))
INNER_SUMS = 3
DAMPING = 0.8
SWEEPS = 3
STEP = 0.8
HIGHEST = lax.Precision.HIGHEST
F32 = jnp.float32
BF16 = jnp.bfloat16
SMALL_ROWS = 2


def dot(a, b):
    return jnp.dot(a, b, precision=HIGHEST, preferred_element_type=F32)


def kernel(
    n,
    source_ref,
    links_ref,
    prol_ref,
    inverse_ref,
    solution_ref,
    residual_ref,
    raw,
    lcat,
    weights,
    field,
    outgoing,
    halo,
    prol_halo,
    coarse_out,
    coarse_halo,
    acc,
    stage,
    gather,
    small_stage,
    small,
    rall,
    link_sem,
    halo_send,
    halo_recv,
    near_send,
    near_recv,
    gather_send,
    gather_recv,
    small_send,
    small_recv,
):
    me = lax.axis_index("ta")
    sites, rhs, comps = source_ref.shape[1:]
    ks = prol_ref.shape[2]
    width = sites * rhs
    right, left = lax.rem(me + 1, n), lax.rem(me + n - 1, n)

    barrier = pltpu.get_barrier_semaphore()

    def greet(d, carry):
        pl.semaphore_signal(barrier, inc=1, device_id={"ta": lax.rem(me + d, n)})
        return carry

    lax.fori_loop(1, n, greet, 0)
    for s in range(sites):
        pltpu.make_async_copy(links_ref.at[0, s], raw.at[s], link_sem.at[s]).start()

    lane_site = lax.broadcasted_iota(jnp.int32, (1, width), 1) // rhs
    even = lane_site % 2 == 0

    def over_sites(x):
        shift = rhs
        while shift < width:
            x = x + pltpu.roll(x, shift, 1)
            shift *= 2
        return x

    prol = prol_ref[0].reshape(sites * ks, comps)
    row_site = lax.broadcasted_iota(jnp.int32, (sites * ks, width), 0) // ks
    diagonal = row_site == lax.broadcasted_iota(jnp.int32, (sites * ks, width), 1) // rhs

    def two_parts(a):
        hi = a.astype(BF16)
        return hi, (a - hi.astype(F32)).astype(BF16)

    prol_parts = jnp.concatenate(two_parts(prol), axis=0)
    inverse_parts = jnp.concatenate(two_parts(inverse_ref[...]), axis=0)

    def dot_parts(a, b):
        p = jnp.dot(a, b, preferred_element_type=F32)
        rows = a.shape[0] // 2
        return p[:rows, :width] + p[:rows, width:] + p[rows:, :width]

    def restrict():
        full = jnp.where(diagonal, dot_parts(prol_parts, weights[:comps]), 0.0)
        return functools.reduce(jnp.add, [full[s * ks : (s + 1) * ks] for s in range(sites)])

    def products(pairs, rows=1):
        packed = []
        for at in range(0, rows * sites, sites):
            row = jnp.zeros((1, width), F32)
            for i, (a, b) in enumerate(pairs[at : at + sites]):
                row = jnp.where(lane_site == i, over_sites(jnp.sum(a * b, axis=0, keepdims=True)), row)
            packed.append(row)
        return packed[0] if rows == 1 else jnp.concatenate(packed, axis=0)

    block = comps // sites

    def send_site(r, s, v):
        message = jnp.zeros((block, width), F32)
        for q in range(sites):
            moved = pltpu.roll(
                v[q * block : (q + 1) * block], lax.rem(q + sites - s, sites) * rhs, 1
            )
            message = jnp.where(lane_site == q, moved, message)
        outgoing[r, s] = message
        for side, to in ((0, left), (1, right)):
            pltpu.make_async_remote_copy(
                src_ref=outgoing.at[r, s],
                dst_ref=halo.at[r, side, s],
                send_sem=halo_send.at[r, side],
                recv_sem=halo_recv.at[r, side, s],
                device_id={"ta": to},
            ).start()

    def send_field(r, f):
        def one(s, carry):
            send_site(r, s, field[f])
            return carry

        lax.fori_loop(0, sites, one, 0)

    def near(k, src, dst):
        return [
            pltpu.make_async_remote_copy(
                src_ref=src,
                dst_ref=dst.at[side],
                send_sem=near_send.at[k, side],
                recv_sem=near_recv.at[k, side],
                device_id={"ta": to},
            )
            for side, to in ((0, left), (1, right))
        ]

    def exchange(k, value, staged, slots, send_sem, recv_sem):
        staged[k] = value
        slots[k, me] = value

        def one(d, carry):
            pltpu.make_async_remote_copy(
                src_ref=staged.at[k],
                dst_ref=slots.at[k, me],
                send_sem=send_sem.at[k],
                recv_sem=recv_sem.at[k],
                device_id={"ta": lax.rem(me + d, n)},
            ).start()
            return carry

        lax.fori_loop(1, n, one, 0)
        return pltpu.make_async_remote_copy(
            src_ref=slots.at[k, pl.ds(0, n - 1)],
            dst_ref=slots.at[k, pl.ds(0, n - 1)],
            send_sem=send_sem.at[k],
            recv_sem=recv_sem.at[k],
            device_id={"ta": right},
        )

    pending = []

    def exchange_large(k, value):
        c = exchange(k, value, stage, gather, gather_send, gather_recv)
        pending.append(c)
        return c

    def exchange_small(k, value):
        c = exchange(k, value, small_stage, small, small_send, small_recv)
        pending.append(c)
        return c

    def load_weights(at, v):
        hi = v.astype(BF16)
        lo = (v - hi.astype(F32)).astype(BF16)
        weights[at * comps : (at + 1) * comps, :width] = hi
        weights[at * comps : (at + 1) * comps, width:] = lo

    def product(s, lo_k, hi_k):
        k = slice(lo_k * comps, hi_k * comps)
        p = jnp.dot(lcat[s, :comps, k], weights[k], preferred_element_type=F32)
        q = jnp.dot(lcat[s, comps:, k], weights[k, :width], preferred_element_type=F32)
        return p[:, :width] + p[:, width:] + q

    def load_inner(f):
        v = field[f]
        load_weights(0, v)
        load_weights(1, pltpu.roll(v, width // 2, 1))
        load_weights(2, jnp.where(even, pltpu.roll(v, width - rhs, 1), pltpu.roll(v, rhs, 1)))

    def inner():
        def site(s, carry):
            acc[...] = jnp.where(lane_site == s, product(s, 0, INNER_SUMS), acc[...])
            return carry

        lax.fori_loop(0, sites, site, 0, unroll=True)

    def outer(r, f, to, of_field, of_links, send=None):
        def site(s, carry):
            if r is not None:
                for side in range(2):
                    pltpu.make_async_remote_copy(
                        src_ref=outgoing.at[r, s],
                        dst_ref=halo.at[r, side, s],
                        send_sem=halo_send.at[r, side],
                        recv_sem=halo_recv.at[r, side, s],
                        device_id={"ta": left},
                    ).wait_recv()
                    m = halo[r, side, s]
                    load_weights(
                        INNER_SUMS + side,
                        jnp.concatenate(
                            [
                                pltpu.roll(m, lax.rem(s + sites - q, sites) * rhs, 1)
                                for q in range(sites)
                            ],
                            axis=0,
                        ),
                    )
            new = of_field * field[f] + of_links * (acc[...] + product(s, INNER_SUMS, len(LINK_SUMS)))
            field[to] = jnp.where(lane_site == s, new, field[to])
            if send is not None:
                send_site(send, s, new)
            return carry

        lax.fori_loop(0, sites, site, 0)

    def sweeps(gram):
        c = [jnp.ones((1, width), F32)]
        x = [jnp.zeros((1, width), F32)] * SWEEPS
        for _ in range(SWEEPS):
            size = len(c)
            d = [(c[0]) / STEP] + [(c[i] - c[i - 1]) / STEP for i in range(1, size)] + [-c[-1] / STEP]
            gd = [
                functools.reduce(jnp.add, [gram(i, j) * d[j] for j in range(size + 1)])
                for i in range(size + 1)
            ]
            across = functools.reduce(jnp.add, [gd[i] * c[i] for i in range(size)])
            squared = functools.reduce(jnp.add, [gd[i] * d[i] for i in range(size + 1)])
            factor = DAMPING * across / squared
            x = [x[i] + factor * c[i] if i < size else x[i] for i in range(SWEEPS)]
            c = [c[i] - factor * d[i] if i < size else -factor * d[i] for i in range(size + 1)]
        return c, x

    def combine(coefficients, fields):
        return functools.reduce(jnp.add, [a * field[f] for a, f in zip(coefficients, fields)])

    field[0] = source_ref[0].reshape(width, comps).T
    pl.semaphore_wait(barrier, n - 1)
    send_field(0, 0)
    prol_copies = near(0, prol_ref.at[0], prol_halo)
    for copy in prol_copies:
        copy.start()

    def prepare(s, carry):
        pltpu.make_async_copy(links_ref.at[0, s], raw.at[s], link_sem.at[s]).wait()
        for at, members in enumerate(LINK_SUMS):
            total = functools.reduce(jnp.add, [raw[s, m] for m in members])
            hi = total.astype(BF16)
            lo = (total - hi.astype(F32)).astype(BF16)
            lcat[s, :comps, at * comps : (at + 1) * comps] = hi
            lcat[s, comps:, at * comps : (at + 1) * comps] = lo
        return carry

    lax.fori_loop(0, sites, prepare, 0)
    for k in range(SWEEPS + 1):
        load_inner(k)
        value = jnp.concatenate(
            [restrict(), products([(field[k], field[i]) for i in range(k + 1)])], axis=0
        )
        exchange_large(k, value)
        inner()
        outer(k, k, k + 1, 1.0 - STEP, -STEP, k + 1 if k < SWEEPS else None)
    for k in range(SWEEPS + 1):
        pending[k].wait_recv()

    def total_of(slots, k, at, rows):
        def one(t, total):
            return total + slots[k, t, at : at + rows]

        return lax.fori_loop(0, n, one, jnp.zeros((rows, width), F32))

    def unpack(total, i):
        row = total[i // sites : i // sites + 1]
        return over_sites(jnp.where(lane_site == i % sites, row, 0.0))

    totals = [total_of(gather, k, ks, 1) for k in range(SWEEPS + 1)]
    grams = {(k, i): unpack(totals[k], i) for k in range(SWEEPS + 1) for i in range(k + 1)}
    c, x = sweeps(lambda i, j: grams[max(i, j), min(i, j)])

    def spread(t, carry):
        r = functools.reduce(jnp.add, [c[k] * gather[k, t, :ks] for k in range(SWEEPS + 1)])
        for s in range(sites):
            hi, lo = two_parts(jnp.where(lane_site == s, r, 0.0))
            at = pl.ds(pl.multiple_of((t * sites + s) * ks, ks), ks)
            rall[at, :width] = hi
            rall[at, width:] = lo
        return carry

    lax.fori_loop(0, n, spread, 0)
    coarse = over_sites(dot_parts(inverse_parts, rall[...]))
    coarse = jnp.where(diagonal, coarse, 0.0)
    compact = functools.reduce(jnp.add, [coarse[s * ks : (s + 1) * ks] for s in range(sites)])
    coarse_out[...] = compact
    coarse_copies = near(1, coarse_out, coarse_halo)
    for copy in coarse_copies:
        copy.start()
    field[5] = dot(prol.T, coarse)
    load_inner(5)
    inner()
    field[7] = combine(c, range(SWEEPS + 1))
    field[8] = combine(c, range(1, SWEEPS + 2))
    field[9] = combine(x, range(SWEEPS))
    for side in range(2):
        prol_copies[side].wait_recv()
        coarse_copies[side].wait_recv()
        there = jnp.where(diagonal, jnp.concatenate([coarse_halo[side]] * sites, axis=0), 0.0)
        vectors = prol_halo[side].reshape(sites * ks, comps)
        load_weights(INNER_SUMS + side, dot(vectors.T, there))
    outer(None, 5, 6, 1.0, 1.0, 4)
    exchange_small(0, products([(field[6], field[7]), (field[6], field[6])], SMALL_ROWS))
    load_inner(6)
    inner()
    outer(4, 6, 14, 1.0 - STEP, -STEP)
    pending[-1].wait_recv()
    pair = total_of(small, 0, 0, SMALL_ROWS)
    g = unpack(pair, 0) / unpack(pair, 1)

    field[11] = field[8] - g * field[14]
    send_field(5, 11)
    field[10] = field[7] - g * field[6]
    field[9] = field[9] + g * field[5]
    load_inner(11)
    inner()
    outer(5, 11, 12, 1.0 - STEP, -STEP, 6)
    early = [(i, j) for i in range(3) for j in range(i + 1)]
    late = [(3, j) for j in range(4)]
    exchange_small(1, products([(field[10 + i], field[10 + j]) for i, j in early], SMALL_ROWS))
    load_inner(12)
    inner()
    outer(6, 12, 13, 1.0 - STEP, -STEP)
    exchange_small(2, products([(field[10 + i], field[10 + j]) for i, j in late], SMALL_ROWS))
    pending[-2].wait_recv()
    pending[-1].wait_recv()
    sums = [total_of(small, 1, 0, SMALL_ROWS), total_of(small, 2, 0, SMALL_ROWS)]
    grams_after = {pair: unpack(sums[0], early.index(pair)) for pair in early}
    grams_after.update({pair: unpack(sums[1], late.index(pair)) for pair in late})

    def gram(i, j):
        return grams_after[max(i, j), min(i, j)]

    c, x = sweeps(gram)
    residual_ref[...] = combine(c, range(10, 14))
    solution_ref[...] = field[9] + combine(x, range(10, 13))
    for r in range(halo.shape[0]):
        for side in range(2):
            pltpu.make_async_remote_copy(
                src_ref=outgoing.at[r],
                dst_ref=halo.at[r, side],
                send_sem=halo_send.at[r, side],
                recv_sem=halo_recv.at[r, side, 0],
                device_id={"ta": left},
            ).wait_send()
    for copy in pending + prol_copies + coarse_copies:
        copy.wait_send()


def turn(*refs):
    for column, row in zip(refs[:2], refs[2:]):
        row[0] = column[...].T.reshape(row.shape[1:])


def local(source, links, prolongator, coarse_inverse):
    n = lax.axis_size("ta")
    _, sites, rhs, comps = source.shape
    ks = prolongator.shape[2]
    width = sites * rhs
    sums = len(LINK_SUMS)
    vmem = pl.BlockSpec(memory_space=pltpu.VMEM)
    dma = pltpu.SemaphoreType.DMA
    columns = pl.pallas_call(
        functools.partial(kernel, n),
        out_shape=(jax.ShapeDtypeStruct((comps, width), F32),) * 2,
        in_specs=[vmem, pl.BlockSpec(memory_space=pl.ANY), vmem, vmem],
        out_specs=(vmem, vmem),
        scratch_shapes=[
            pltpu.VMEM(links.shape[1:], F32),
            pltpu.VMEM((sites, 2 * comps, sums * comps), BF16),
            pltpu.VMEM((sums * comps, 2 * width), BF16),
            pltpu.VMEM((15, comps, width), F32),
            pltpu.VMEM((7, sites, comps // sites, width), F32),
            pltpu.VMEM((7, 2, sites, comps // sites, width), F32),
            pltpu.VMEM((2, *prolongator.shape[1:]), F32),
            pltpu.VMEM((ks, width), F32),
            pltpu.VMEM((2, ks, width), F32),
            pltpu.VMEM((comps, width), F32),
            pltpu.VMEM((SWEEPS + 1, ks + 1, width), F32),
            pltpu.VMEM((SWEEPS + 1, n, ks + 1, width), F32),
            pltpu.VMEM((3, SMALL_ROWS, width), F32),
            pltpu.VMEM((3, n, SMALL_ROWS, width), F32),
            pltpu.VMEM((n * sites * ks, 2 * width), BF16),
            dma((sites,)),
            dma((7, 2)),
            dma((7, 2, sites)),
            dma((2, 2)),
            dma((2, 2)),
            dma((SWEEPS + 1,)),
            dma((SWEEPS + 1,)),
            dma((3,)),
            dma((3,)),
        ],
        compiler_params=pltpu.CompilerParams(
            collective_id=0, has_side_effects=True, vmem_limit_bytes=60 * 1024 * 1024
        ),
    )(source, links, prolongator, coarse_inverse)
    return pl.pallas_call(
        turn,
        out_shape=(jax.ShapeDtypeStruct(source.shape, F32),) * 2,
        in_specs=[vmem, vmem],
        out_specs=(vmem, vmem),
    )(*columns)


def solution(mesh):
    return jax.shard_map(
        local,
        mesh=mesh,
        in_specs=(
            P(("groups", "ta"), None, None, None),
            P("ta", None, None, None, None),
            P("ta", None, None, None),
            P("ta", None),
        ),
        out_specs=(P(("groups", "ta"), None, None, None), P(("groups", "ta"), None, None, None)),
        check_vma=False,
    )
```

profile of v0, /device:TPU:0, one launch (start us, length us, event | category | flops | bytes accessed | tf_op | source)
XLA Modules:
  0.0 59.2 jit_solution(13170770401868453242)
XLA Ops:
  0.6 56.8 %shard_map.59 = (f32[256,128]{1,0:T(8,128)}, f32[256,128]{1,0:T(8,128)}) custom-call(f32[1,4,32,256]{3,2,1,0:T(8,128)} %source_ref.1, f32[1,4,9,256,256]{4,3,2,1,0:T(8,128)} %links_ref.1, f32[1,4,16,256]{3,2,1,0:T(8,128)} %prol_ref.1, f32[64,1024]{1,0:T(8,128)} %inverse_ref.1), custom_call_target="tpu_custom_call" | custom-call | tf_op jit(solution)/shard_map/pallas_call | solution.py:394
  57.4 1.8 %shard_map.60 = (f32[1,4,32,256]{3,2,1,0:T(8,128)}, f32[1,4,32,256]{3,2,1,0:T(8,128)}) custom-call(f32[256,128]{1,0:T(8,128)} %get-tuple-element.4.refs_0_, f32[256,128]{1,0:T(8,128)} %get-tuple-element.5.refs_1_), custom_call_target="tpu_custom_call" | custom-call | tf_op jit(solution)/shard_map/pallas_call | solution.py:429
where the time goes:
time: 59.3 us; the launch traced here: 59.2 us
  Pallas kernels  58.5 us (99%)
  between operations  0.64 us (1%)
    pallas_call x1, Pallas kernels, local(): pl.pallas_call(functools.partial(kernel, n), out_shape=(jax.ShapeDtypeStr...  56.8 us
    pallas_call x1, Pallas kernels, local(): pl.pallas_call(turn, out_shape=(jax.ShapeDtypeStruct(source.shape, F32),)...  1.77 us

commit v1 on v0

--- a/solution.py
+++ b/solution.py
@@ -30,6 +30,9 @@
     inverse_ref,
     solution_ref,
     residual_ref,
+    source_in,
+    prol_in,
+    inverse_in,
     raw,
     lcat,
     weights,
@@ -45,6 +48,9 @@
     small_stage,
     small,
     rall,
+    gcat,
+    xcat,
+    input_sem,
     link_sem,
     halo_send,
     halo_recv,
@@ -68,8 +74,17 @@
         return carry
 
     lax.fori_loop(1, n, greet, 0)
+    inputs = [
+        pltpu.make_async_copy(hbm, vmem, input_sem.at[i])
+        for i, (hbm, vmem) in enumerate(
+            ((source_ref, source_in), (prol_ref, prol_in), (inverse_ref, inverse_in))
+        )
+    ]
+    inputs[0].start()
+    inputs[1].start()
     for s in range(sites):
         pltpu.make_async_copy(links_ref.at[0, s], raw.at[s], link_sem.at[s]).start()
+    inputs[2].start()
 
     lane_site = lax.broadcasted_iota(jnp.int32, (1, width), 1) // rhs
     even = lane_site % 2 == 0
@@ -81,7 +96,6 @@
             shift *= 2
         return x
 
-    prol = prol_ref[0].reshape(sites * ks, comps)
     row_site = lax.broadcasted_iota(jnp.int32, (sites * ks, width), 0) // ks
     diagonal = row_site == lax.broadcasted_iota(jnp.int32, (sites * ks, width), 1) // rhs
 
@@ -89,8 +103,6 @@
         hi = a.astype(BF16)
         return hi, (a - hi.astype(F32)).astype(BF16)
 
-    prol_parts = jnp.concatenate(two_parts(prol), axis=0)
-    inverse_parts = jnp.concatenate(two_parts(inverse_ref[...]), axis=0)
 
     def dot_parts(a, b):
         p = jnp.dot(a, b, preferred_element_type=F32)
@@ -238,32 +250,46 @@
 
         lax.fori_loop(0, sites, site, 0)
 
-    def sweeps(gram):
+    def image_of(c):
+        last = len(c) - 1
+        inside = [(c[i] - c[i - 1]) / STEP for i in range(1, last + 1)]
+        return [c[0] / STEP] + inside + [-c[last] / STEP]
+
+    def factor_of(gram, c, d):
+        gd = [
+            functools.reduce(jnp.add, [gram(i, j) * d[j] for j in range(len(d))])
+            for i in range(len(d))
+        ]
+        across = functools.reduce(jnp.add, [gd[i] * c[i] for i in range(len(c))])
+        squared = functools.reduce(jnp.add, [gd[i] * d[i] for i in range(len(d))])
+        return DAMPING * across / squared
+
+    def advance(c, x, d, factor):
+        x = [x[i] + factor * c[i] if i < len(c) else x[i] for i in range(SWEEPS)]
+        return [c[i] - factor * d[i] if i < len(c) else -factor * d[i] for i in range(len(d))], x
+
+    def sweeps(gram, count):
         c = [jnp.ones((1, width), F32)]
         x = [jnp.zeros((1, width), F32)] * SWEEPS
-        for _ in range(SWEEPS):
-            size = len(c)
-            d = [(c[0]) / STEP] + [(c[i] - c[i - 1]) / STEP for i in range(1, size)] + [-c[-1] / STEP]
-            gd = [
-                functools.reduce(jnp.add, [gram(i, j) * d[j] for j in range(size + 1)])
-                for i in range(size + 1)
-            ]
-            across = functools.reduce(jnp.add, [gd[i] * c[i] for i in range(size)])
-            squared = functools.reduce(jnp.add, [gd[i] * d[i] for i in range(size + 1)])
-            factor = DAMPING * across / squared
-            x = [x[i] + factor * c[i] if i < size else x[i] for i in range(SWEEPS)]
-            c = [c[i] - factor * d[i] if i < size else -factor * d[i] for i in range(size + 1)]
+        for _ in range(count):
+            d = image_of(c)
+            c, x = advance(c, x, d, factor_of(gram, c, d))
         return c, x
 
     def combine(coefficients, fields):
         return functools.reduce(jnp.add, [a * field[f] for a, f in zip(coefficients, fields)])
 
-    field[0] = source_ref[0].reshape(width, comps).T
+    half = sites * ks
+    inputs[0].wait()
+    field[0] = source_in[0].reshape(width, comps).T
     pl.semaphore_wait(barrier, n - 1)
     send_field(0, 0)
-    prol_copies = near(0, prol_ref.at[0], prol_halo)
+    inputs[1].wait()
+    prol_copies = near(0, prol_in.at[0], prol_halo)
     for copy in prol_copies:
         copy.start()
+    prol = prol_in[0].reshape(half, comps)
+    prol_parts = jnp.concatenate(two_parts(prol), axis=0)
 
     def prepare(s, carry):
         pltpu.make_async_copy(links_ref.at[0, s], raw.at[s], link_sem.at[s]).wait()
@@ -282,58 +308,131 @@
             [restrict(), products([(field[k], field[i]) for i in range(k + 1)])], axis=0
         )
         exchange_large(k, value)
+        if k == SWEEPS:
+            send_field(k, k)
         inner()
-        outer(k, k, k + 1, 1.0 - STEP, -STEP, k + 1 if k < SWEEPS else None)
-    for k in range(SWEEPS + 1):
-        pending[k].wait_recv()
+        if k < SWEEPS:
+            outer(k, k, k + 1, 1.0 - STEP, -STEP, k + 1 if k + 1 < SWEEPS else None)
+
+    for copy in prol_copies:
+        copy.wait_recv()
+
+    def columns_of(p):
+        hi = p.astype(BF16).astype(F32)
+        return jnp.concatenate([hi, p - hi], axis=0).T.astype(BF16)
+
+    bases = [columns_of(p.reshape(half, comps)) for p in (prol, prol_halo[0], prol_halo[1])]
+    vectors = jnp.concatenate([prol, prol], axis=0).T
+    g_lane = lax.broadcasted_iota(jnp.int32, (1, 2 * half), 1)
+    g_site, g_low = lax.rem(g_lane, half) // ks, g_lane < half
+
+    def operate_on_bases(s, carry):
+        def times(m, base):
+            k = slice(m * comps, (m + 1) * comps)
+            r = jnp.dot(lcat[s, :comps, k], base, preferred_element_type=F32)
+            r = r + jnp.dot(lcat[s, comps:, k], base, preferred_element_type=F32)
+            return r + pltpu.roll(r, half, 1)
+
+        across = s + 1 - 2 * lax.rem(s, 2)
+        own = jnp.where(g_site == s, vectors + times(0, bases[0]), 0.0)
+        own = jnp.where(g_site == lax.rem(s + sites // 2, sites), times(1, bases[0]), own)
+        own = jnp.where(g_site == across, times(2, bases[0]), own)
+        ahead = jnp.where(g_site == s, times(3, bases[1]), 0.0)
+        behind = jnp.where((g_site == s) & g_low, times(4, bases[2]), 0.0)
+        for at, value in enumerate((jnp.where(g_low, own, ahead), behind)):
+            hi, lo = two_parts(value)
+            lanes = slice(at * 2 * half, (at + 1) * 2 * half)
+            gcat[s, :comps, lanes] = hi
+            gcat[s, comps:, lanes] = lo
+        return carry
+
+    lax.fori_loop(0, sites, operate_on_bases, 0)
+    inputs[2].wait()
+    inverse_parts = jnp.concatenate(two_parts(inverse_in[...]), axis=0)
 
     def total_of(slots, k, at, rows):
-        def one(t, total):
-            return total + slots[k, t, at : at + rows]
-
-        return lax.fori_loop(0, n, one, jnp.zeros((rows, width), F32))
+        return jnp.sum(slots[k, :, at : at + rows, :], axis=0)
 
     def unpack(total, i):
         row = total[i // sites : i // sites + 1]
         return over_sites(jnp.where(lane_site == i % sites, row, 0.0))
 
-    totals = [total_of(gather, k, ks, 1) for k in range(SWEEPS + 1)]
-    grams = {(k, i): unpack(totals[k], i) for k in range(SWEEPS + 1) for i in range(k + 1)}
-    c, x = sweeps(lambda i, j: grams[max(i, j), min(i, j)])
-
-    def spread(t, carry):
-        r = functools.reduce(jnp.add, [c[k] * gather[k, t, :ks] for k in range(SWEEPS + 1)])
-        for s in range(sites):
-            hi, lo = two_parts(jnp.where(lane_site == s, r, 0.0))
-            at = pl.ds(pl.multiple_of((t * sites + s) * ks, ks), ks)
-            rall[at, :width] = hi
-            rall[at, width:] = lo
-        return carry
-
-    lax.fori_loop(0, n, spread, 0)
-    coarse = over_sites(dot_parts(inverse_parts, rall[...]))
-    coarse = jnp.where(diagonal, coarse, 0.0)
-    compact = functools.reduce(jnp.add, [coarse[s * ks : (s + 1) * ks] for s in range(sites)])
+    def solve_coarse(coefficients):
+        def spread(t, carry):
+            r = functools.reduce(
+                jnp.add, [a * gather[k, t, :ks] for k, a in enumerate(coefficients)]
+            )
+            for s in range(sites):
+                hi, lo = two_parts(jnp.where(lane_site == s, r, 0.0))
+                at = pl.ds(pl.multiple_of((t * sites + s) * ks, ks), ks)
+                rall[at, :width] = hi
+                rall[at, width:] = lo
+            return carry
+
+        lax.fori_loop(0, n, spread, 0)
+        return over_sites(dot_parts(inverse_parts, rall[...]))
+
+    def store_coarse(at, x):
+        hi, lo = two_parts(x)
+        xcat[at * half : (at + 1) * half, :width] = hi
+        xcat[at * half : (at + 1) * half, width:] = lo
+
+    grams = {}
+
+    def gram(i, j):
+        return grams[max(i, j), min(i, j)]
+
+    def read_grams(k):
+        pending[k].wait_recv()
+        total = total_of(gather, k, ks, 1)
+        grams.update({(k, i): unpack(total, i) for i in range(k + 1)})
+
+    for k in range(SWEEPS):
+        read_grams(k)
+    c, x = sweeps(gram, SWEEPS - 1)
+    d = image_of(c)
+    before = solve_coarse(c)
+    xcat[3 * half :] = jnp.zeros((xcat.shape[0] - 3 * half, 2 * width), BF16)
+    read_grams(SWEEPS)
+    factor = factor_of(gram, c, d)
+    coarse = before - factor * solve_coarse(d)
+    compact = functools.reduce(
+        jnp.add,
+        [jnp.where(lane_site == s, coarse[s * ks : (s + 1) * ks], 0.0) for s in range(sites)],
+    )
     coarse_out[...] = compact
     coarse_copies = near(1, coarse_out, coarse_halo)
     for copy in coarse_copies:
         copy.start()
-    field[5] = dot(prol.T, coarse)
-    load_inner(5)
-    inner()
+    c, x = advance(c, x, d, factor)
+    store_coarse(0, coarse)
+    outer(SWEEPS, SWEEPS, SWEEPS + 1, 1.0 - STEP, -STEP)
     field[7] = combine(c, range(SWEEPS + 1))
-    field[8] = combine(c, range(1, SWEEPS + 2))
-    field[9] = combine(x, range(SWEEPS))
     for side in range(2):
-        prol_copies[side].wait_recv()
         coarse_copies[side].wait_recv()
-        there = jnp.where(diagonal, jnp.concatenate([coarse_halo[side]] * sites, axis=0), 0.0)
-        vectors = prol_halo[side].reshape(sites * ks, comps)
-        load_weights(INNER_SUMS + side, dot(vectors.T, there))
-    outer(None, 5, 6, 1.0, 1.0, 4)
+        there = coarse_halo[side]
+        store_coarse(
+            1 + side,
+            jnp.concatenate(
+                [over_sites(jnp.where(lane_site == s, there, 0.0)) for s in range(sites)], axis=0
+            ),
+        )
+
+    def operate_on_coarse(s, carry):
+        p = jnp.dot(gcat[s, :comps], xcat[...], preferred_element_type=F32)
+        q = jnp.dot(gcat[s, comps:], xcat[:, :width], preferred_element_type=F32)
+        new = p[:, :width] + p[:, width:] + q
+        field[6] = jnp.where(lane_site == s, new, field[6])
+        send_site(4, s, new)
+        return carry
+
+    lax.fori_loop(0, sites, operate_on_coarse, 0)
     exchange_small(0, products([(field[6], field[7]), (field[6], field[6])], SMALL_ROWS))
     load_inner(6)
     inner()
+    field[8] = combine(c, range(1, SWEEPS + 2))
+    field[9] = combine(x, range(SWEEPS))
+    field[5] = dot(prol.T, jnp.where(diagonal, coarse, 0.0))
     outer(4, 6, 14, 1.0 - STEP, -STEP)
     pending[-1].wait_recv()
     pair = total_of(small, 0, 0, SMALL_ROWS)
@@ -353,18 +452,6 @@
     inner()
     outer(6, 12, 13, 1.0 - STEP, -STEP)
     exchange_small(2, products([(field[10 + i], field[10 + j]) for i, j in late], SMALL_ROWS))
-    pending[-2].wait_recv()
-    pending[-1].wait_recv()
-    sums = [total_of(small, 1, 0, SMALL_ROWS), total_of(small, 2, 0, SMALL_ROWS)]
-    grams_after = {pair: unpack(sums[0], early.index(pair)) for pair in early}
-    grams_after.update({pair: unpack(sums[1], late.index(pair)) for pair in late})
-
-    def gram(i, j):
-        return grams_after[max(i, j), min(i, j)]
-
-    c, x = sweeps(gram)
-    residual_ref[...] = combine(c, range(10, 14))
-    solution_ref[...] = field[9] + combine(x, range(10, 13))
     for r in range(halo.shape[0]):
         for side in range(2):
             pltpu.make_async_remote_copy(
@@ -374,8 +461,20 @@
                 recv_sem=halo_recv.at[r, side, 0],
                 device_id={"ta": left},
             ).wait_send()
-    for copy in pending + prol_copies + coarse_copies:
+    for copy in pending[:-1] + prol_copies + coarse_copies:
         copy.wait_send()
+    pending[-2].wait_recv()
+    total = total_of(small, 1, 0, SMALL_ROWS)
+    grams = {pair: unpack(total, early.index(pair)) for pair in early}
+    c, x = sweeps(gram, SWEEPS - 1)
+    d = image_of(c)
+    pending[-1].wait_recv()
+    total = total_of(small, 2, 0, SMALL_ROWS)
+    grams.update({pair: unpack(total, late.index(pair)) for pair in late})
+    c, x = advance(c, x, d, factor_of(gram, c, d))
+    residual_ref[...] = combine(c, range(10, 14))
+    solution_ref[...] = field[9] + combine(x, range(10, 13))
+    pending[-1].wait_send()
 
 
 def turn(*refs):
@@ -394,9 +493,12 @@
     columns = pl.pallas_call(
         functools.partial(kernel, n),
         out_shape=(jax.ShapeDtypeStruct((comps, width), F32),) * 2,
-        in_specs=[vmem, pl.BlockSpec(memory_space=pl.ANY), vmem, vmem],
+        in_specs=[pl.BlockSpec(memory_space=pl.ANY)] * 4,
         out_specs=(vmem, vmem),
         scratch_shapes=[
+            pltpu.VMEM(source.shape, F32),
+            pltpu.VMEM(prolongator.shape, F32),
+            pltpu.VMEM(coarse_inverse.shape, F32),
             pltpu.VMEM(links.shape[1:], F32),
             pltpu.VMEM((sites, 2 * comps, sums * comps), BF16),
             pltpu.VMEM((sums * comps, 2 * width), BF16),
@@ -412,6 +514,9 @@
             pltpu.VMEM((3, SMALL_ROWS, width), F32),
             pltpu.VMEM((3, n, SMALL_ROWS, width), F32),
             pltpu.VMEM((n * sites * ks, 2 * width), BF16),
+            pltpu.VMEM((sites, 2 * comps, 4 * sites * ks), BF16),
+            pltpu.VMEM((4 * sites * ks, 2 * width), BF16),
+            dma((3,)),
             dma((sites,)),
             dma((7, 2)),
             dma((7, 2, sites)),

time: 59.3 us -> 57.9 us (0.976)
  Pallas kernels: 58.5 us -> 57.1 us
    pallas_call x1, Pallas kernels: 56.8 us -> 55.4 us  [local(): pl.pallas_call(functools.partial(kernel, n), out_shape=(jax.ShapeDtypeStr...]
where the time goes in v1:
time: 57.9 us; the launch traced here: 57.8 us
  Pallas kernels  57.1 us (99%)
  between operations  0.64 us (1%)
    pallas_call x1, Pallas kernels, local(): pl.pallas_call(functools.partial(kernel, n), out_shape=(jax.ShapeDtypeStr...  55.4 us
    pallas_call x1, Pallas kernels, local(): pl.pallas_call(turn, out_shape=(jax.ShapeDtypeStruct(source.shape, F32),)...  1.77 us

profile of v1, /device:TPU:0, one launch (start us, length us, event | category | flops | bytes accessed | tf_op | source)
XLA Modules:
  0.0 57.8 jit_solution(17603763224532254032)
XLA Ops:
  0.6 55.4 %shard_map.59 = (f32[256,128]{1,0:T(8,128)}, f32[256,128]{1,0:T(8,128)}) custom-call(f32[1,4,32,256]{3,2,1,0:T(8,128)} %source_ref.1, f32[1,4,9,256,256]{4,3,2,1,0:T(8,128)} %links_ref.1, f32[1,4,16,256]{3,2,1,0:T(8,128)} %prol_ref.1, f32[64,1024]{1,0:T(8,128)} %inverse_ref.1), custom_call_target="tpu_custom_call" | custom-call | tf_op jit(solution)/shard_map/pallas_call | solution.py:493
  56.0 1.8 %shard_map.60 = (f32[1,4,32,256]{3,2,1,0:T(8,128)}, f32[1,4,32,256]{3,2,1,0:T(8,128)}) custom-call(f32[256,128]{1,0:T(8,128)} %get-tuple-element.4.refs_0_, f32[256,128]{1,0:T(8,128)} %get-tuple-element.5.refs_1_), custom_call_target="tpu_custom_call" | custom-call | tf_op jit(solution)/shard_map/pallas_call | solution.py:534

commit v2 on v1

--- a/solution.py
+++ b/solution.py
@@ -58,6 +58,8 @@
     near_recv,
     gather_send,
     gather_recv,
+    share_send,
+    share_recv,
     small_send,
     small_recv,
 ):
@@ -185,10 +187,46 @@
 
     pending = []
 
+    core, chips = lax.rem(me, 2), n // 2
+    partner = me + 1 - 2 * core
+
+    def gather_copy(k, blocks):
+        return pltpu.make_async_remote_copy(
+            src_ref=gather.at[k, core, blocks],
+            dst_ref=gather.at[k, core, blocks],
+            send_sem=gather_send.at[k],
+            recv_sem=gather_recv.at[k],
+            device_id={"ta": partner},
+        )
+
+    def share_copy(k):
+        return pltpu.make_async_remote_copy(
+            src_ref=gather.at[k, core],
+            dst_ref=gather.at[k, core],
+            send_sem=share_send.at[k],
+            recv_sem=share_recv.at[k],
+            device_id={"ta": partner},
+        )
+
     def exchange_large(k, value):
-        c = exchange(k, value, stage, gather, gather_send, gather_recv)
-        pending.append(c)
-        return c
+        stage[k] = value
+        gather[k, core, me // 2] = value
+
+        def one(d, carry):
+            pltpu.make_async_remote_copy(
+                src_ref=stage.at[k],
+                dst_ref=gather.at[k, core, me // 2],
+                send_sem=gather_send.at[k],
+                recv_sem=gather_recv.at[k],
+                device_id={"ta": lax.rem(me + 2 * d, n)},
+            ).start()
+            return carry
+
+        lax.fori_loop(1, chips, one, 0)
+
+    def share_large(k):
+        gather_copy(k, pl.ds(0, chips - 1)).wait_recv()
+        share_copy(k).start()
 
     def exchange_small(k, value):
         c = exchange(k, value, small_stage, small, small_send, small_recv)
@@ -286,8 +324,6 @@
     send_field(0, 0)
     inputs[1].wait()
     prol_copies = near(0, prol_in.at[0], prol_halo)
-    for copy in prol_copies:
-        copy.start()
     prol = prol_in[0].reshape(half, comps)
     prol_parts = jnp.concatenate(two_parts(prol), axis=0)
 
@@ -309,67 +345,40 @@
         )
         exchange_large(k, value)
         if k == SWEEPS:
-            send_field(k, k)
+            for copy in prol_copies:
+                copy.start()
         inner()
+        if k:
+            share_large(k - 1)
         if k < SWEEPS:
             outer(k, k, k + 1, 1.0 - STEP, -STEP, k + 1 if k + 1 < SWEEPS else None)
 
-    for copy in prol_copies:
-        copy.wait_recv()
-
-    def columns_of(p):
-        hi = p.astype(BF16).astype(F32)
-        return jnp.concatenate([hi, p - hi], axis=0).T.astype(BF16)
-
-    bases = [columns_of(p.reshape(half, comps)) for p in (prol, prol_halo[0], prol_halo[1])]
-    vectors = jnp.concatenate([prol, prol], axis=0).T
-    g_lane = lax.broadcasted_iota(jnp.int32, (1, 2 * half), 1)
-    g_site, g_low = lax.rem(g_lane, half) // ks, g_lane < half
-
-    def operate_on_bases(s, carry):
-        def times(m, base):
-            k = slice(m * comps, (m + 1) * comps)
-            r = jnp.dot(lcat[s, :comps, k], base, preferred_element_type=F32)
-            r = r + jnp.dot(lcat[s, comps:, k], base, preferred_element_type=F32)
-            return r + pltpu.roll(r, half, 1)
-
-        across = s + 1 - 2 * lax.rem(s, 2)
-        own = jnp.where(g_site == s, vectors + times(0, bases[0]), 0.0)
-        own = jnp.where(g_site == lax.rem(s + sites // 2, sites), times(1, bases[0]), own)
-        own = jnp.where(g_site == across, times(2, bases[0]), own)
-        ahead = jnp.where(g_site == s, times(3, bases[1]), 0.0)
-        behind = jnp.where((g_site == s) & g_low, times(4, bases[2]), 0.0)
-        for at, value in enumerate((jnp.where(g_low, own, ahead), behind)):
-            hi, lo = two_parts(value)
-            lanes = slice(at * 2 * half, (at + 1) * 2 * half)
-            gcat[s, :comps, lanes] = hi
-            gcat[s, comps:, lanes] = lo
-        return carry
-
-    lax.fori_loop(0, sites, operate_on_bases, 0)
     inputs[2].wait()
     inverse_parts = jnp.concatenate(two_parts(inverse_in[...]), axis=0)
 
     def total_of(slots, k, at, rows):
-        return jnp.sum(slots[k, :, at : at + rows, :], axis=0)
+        return jnp.sum(slots.at[k][:, at : at + rows, :], axis=0)
 
     def unpack(total, i):
         row = total[i // sites : i // sites + 1]
         return over_sites(jnp.where(lane_site == i % sites, row, 0.0))
 
     def solve_coarse(coefficients):
-        def spread(t, carry):
-            r = functools.reduce(
-                jnp.add, [a * gather[k, t, :ks] for k, a in enumerate(coefficients)]
-            )
-            for s in range(sites):
-                hi, lo = two_parts(jnp.where(lane_site == s, r, 0.0))
-                at = pl.ds(pl.multiple_of((t * sites + s) * ks, ks), ks)
-                rall[at, :width] = hi
-                rall[at, width:] = lo
+        def spread(chip, carry):
+            for half_chip in range(2):
+                r = functools.reduce(
+                    jnp.add,
+                    [a * gather[k, half_chip, chip, :ks] for k, a in enumerate(coefficients)],
+                )
+                for s in range(sites):
+                    hi, lo = two_parts(jnp.where(lane_site == s, r, 0.0))
+                    row = ((2 * chip + half_chip) * sites + s) * ks
+                    at = pl.ds(pl.multiple_of(row, ks), ks)
+                    rall[at, :width] = hi
+                    rall[at, width:] = lo
             return carry
 
-        lax.fori_loop(0, n, spread, 0)
+        lax.fori_loop(0, chips, spread, 0)
         return over_sites(dot_parts(inverse_parts, rall[...]))
 
     def store_coarse(at, x):
@@ -383,8 +392,8 @@
         return grams[max(i, j), min(i, j)]
 
     def read_grams(k):
-        pending[k].wait_recv()
-        total = total_of(gather, k, ks, 1)
+        share_copy(k).wait_recv()
+        total = functools.reduce(jnp.add, [total_of(gather, (k, c), ks, 1) for c in range(2)])
         grams.update({(k, i): unpack(total, i) for i in range(k + 1)})
 
     for k in range(SWEEPS):
@@ -393,6 +402,7 @@
     d = image_of(c)
     before = solve_coarse(c)
     xcat[3 * half :] = jnp.zeros((xcat.shape[0] - 3 * half, 2 * width), BF16)
+    share_large(SWEEPS)
     read_grams(SWEEPS)
     factor = factor_of(gram, c, d)
     coarse = before - factor * solve_coarse(d)
@@ -406,7 +416,40 @@
         copy.start()
     c, x = advance(c, x, d, factor)
     store_coarse(0, coarse)
-    outer(SWEEPS, SWEEPS, SWEEPS + 1, 1.0 - STEP, -STEP)
+    send_field(SWEEPS, SWEEPS)
+    for copy in prol_copies:
+        copy.wait_recv()
+
+    def columns_of(p):
+        hi = p.astype(BF16).astype(F32)
+        return jnp.concatenate([hi, p - hi], axis=0).T.astype(BF16)
+
+    bases = [columns_of(p.reshape(half, comps)) for p in (prol, prol_halo[0], prol_halo[1])]
+    vectors = jnp.concatenate([prol, prol], axis=0).T
+    g_lane = lax.broadcasted_iota(jnp.int32, (1, 2 * half), 1)
+    g_site, g_low = lax.rem(g_lane, half) // ks, g_lane < half
+
+    def operate_on_bases(s, carry):
+        def times(m, base):
+            k = slice(m * comps, (m + 1) * comps)
+            r = jnp.dot(lcat[s, :comps, k], base, preferred_element_type=F32)
+            r = r + jnp.dot(lcat[s, comps:, k], base, preferred_element_type=F32)
+            return r + pltpu.roll(r, half, 1)
+
+        across = s + 1 - 2 * lax.rem(s, 2)
+        own = jnp.where(g_site == s, vectors + times(0, bases[0]), 0.0)
+        own = jnp.where(g_site == lax.rem(s + sites // 2, sites), times(1, bases[0]), own)
+        own = jnp.where(g_site == across, times(2, bases[0]), own)
+        ahead = jnp.where(g_site == s, times(3, bases[1]), 0.0)
+        behind = jnp.where((g_site == s) & g_low, times(4, bases[2]), 0.0)
+        for at, value in enumerate((jnp.where(g_low, own, ahead), behind)):
+            hi, lo = two_parts(value)
+            lanes = slice(at * 2 * half, (at + 1) * 2 * half)
+            gcat[s, :comps, lanes] = hi
+            gcat[s, comps:, lanes] = lo
+        return carry
+
+    lax.fori_loop(0, sites, operate_on_bases, 0)
     field[7] = combine(c, range(SWEEPS + 1))
     for side in range(2):
         coarse_copies[side].wait_recv()
@@ -428,6 +471,7 @@
 
     lax.fori_loop(0, sites, operate_on_coarse, 0)
     exchange_small(0, products([(field[6], field[7]), (field[6], field[6])], SMALL_ROWS))
+    outer(SWEEPS, SWEEPS, SWEEPS + 1, 1.0 - STEP, -STEP)
     load_inner(6)
     inner()
     field[8] = combine(c, range(1, SWEEPS + 2))
@@ -461,6 +505,9 @@
                 recv_sem=halo_recv.at[r, side, 0],
                 device_id={"ta": left},
             ).wait_send()
+    for k in range(SWEEPS + 1):
+        gather_copy(k, pl.ds(0, chips - 1)).wait_send()
+        share_copy(k).wait_send()
     for copy in pending[:-1] + prol_copies + coarse_copies:
         copy.wait_send()
     pending[-2].wait_recv()
@@ -510,7 +557,7 @@
             pltpu.VMEM((2, ks, width), F32),
             pltpu.VMEM((comps, width), F32),
             pltpu.VMEM((SWEEPS + 1, ks + 1, width), F32),
-            pltpu.VMEM((SWEEPS + 1, n, ks + 1, width), F32),
+            pltpu.VMEM((SWEEPS + 1, 2, n // 2, ks + 1, width), F32),
             pltpu.VMEM((3, SMALL_ROWS, width), F32),
             pltpu.VMEM((3, n, SMALL_ROWS, width), F32),
             pltpu.VMEM((n * sites * ks, 2 * width), BF16),
@@ -522,6 +569,8 @@
             dma((7, 2, sites)),
             dma((2, 2)),
             dma((2, 2)),
+            dma((SWEEPS + 1,)),
+            dma((SWEEPS + 1,)),
             dma((SWEEPS + 1,)),
             dma((SWEEPS + 1,)),
             dma((3,)),

time: 57.9 us -> 55 us (0.950)
  Pallas kernels: 57.1 us -> 54.3 us
    pallas_call x1, Pallas kernels: 55.4 us -> 52.5 us  [local(): pl.pallas_call(functools.partial(kernel, n), out_shape=(jax.ShapeDtypeStr...]
where the time goes in v2:
time: 55 us; the launch traced here: 54.9 us
  Pallas kernels  54.3 us (99%)
  between operations  0.64 us (1%)
    pallas_call x1, Pallas kernels, local(): pl.pallas_call(functools.partial(kernel, n), out_shape=(jax.ShapeDtypeStr...  52.5 us
    pallas_call x1, Pallas kernels, local(): pl.pallas_call(turn, out_shape=(jax.ShapeDtypeStruct(source.shape, F32),)...  1.77 us

profile of v2, /device:TPU:0, one launch (start us, length us, event | category | flops | bytes accessed | tf_op | source)
XLA Modules:
  0.0 54.9 jit_solution(4278530981396342361)
XLA Ops:
  0.6 52.5 %shard_map.59 = (f32[256,128]{1,0:T(8,128)}, f32[256,128]{1,0:T(8,128)}) custom-call(f32[1,4,32,256]{3,2,1,0:T(8,128)} %source_ref.1, f32[1,4,9,256,256]{4,3,2,1,0:T(8,128)} %links_ref.1, f32[1,4,16,256]{3,2,1,0:T(8,128)} %prol_ref.1, f32[64,1024]{1,0:T(8,128)} %inverse_ref.1), custom_call_target="tpu_custom_call" | custom-call | tf_op jit(solution)/shard_map/pallas_call | solution.py:540
  53.1 1.8 %shard_map.60 = (f32[1,4,32,256]{3,2,1,0:T(8,128)}, f32[1,4,32,256]{3,2,1,0:T(8,128)}) custom-call(f32[256,128]{1,0:T(8,128)} %get-tuple-element.4.refs_0_, f32[256,128]{1,0:T(8,128)} %get-tuple-element.5.refs_1_), custom_call_target="tpu_custom_call" | custom-call | tf_op jit(solution)/shard_map/pallas_call | solution.py:583

commit v3 on v2

v3 whole, which is shorter than its diff:
```python
import functools

import jax
import jax.numpy as jnp
from jax import lax
from jax.experimental import pallas as pl
from jax.experimental.pallas import tpu as pltpu
from jax.sharding import PartitionSpec as P

LINK_SUMS = ((0, 3, 4), (5, 6), (7, 8), (1,), (2,))
INNER_SUMS = 3
DAMPING = 0.8
SWEEPS = 3
STEP = 0.8
F32 = jnp.float32
BF16 = jnp.bfloat16
SMALL_ROWS = 2


def dot(a, b):
    return jnp.dot(a, b, preferred_element_type=F32)


def dot_rows(a, b):
    return lax.dot_general(a, b, (((1,), (1,)), ((), ())), preferred_element_type=F32)


def two_parts(a):
    hi = a.astype(BF16)
    return hi, (a - hi.astype(F32)).astype(BF16)


def stacked_parts(a):
    return jnp.concatenate(two_parts(a), axis=0)


def fold(a):
    rows = a.shape[0] // 2
    return a[:rows] + a[rows:]


def kernel(
    n,
    source_ref,
    links_ref,
    prol_ref,
    inverse_ref,
    solution_ref,
    residual_ref,
    prol_in,
    inverse_in,
    raw,
    lcat,
    field,
    parts,
    acc,
    halo,
    prol_halo,
    prol_sites,
    images,
    coarse_out,
    coarse_halo,
    stage,
    gather,
    small_stage,
    small,
    rall,
    input_sem,
    link_sem,
    halo_send,
    halo_recv,
    near_send,
    near_recv,
    gather_send,
    gather_recv,
    share_send,
    share_recv,
    small_send,
    small_recv,
):
    me = lax.axis_index("ta")
    sites = links_ref.shape[1]
    width, comps = source_ref.shape
    rhs = width // sites
    half = prol_ref.shape[0]
    ks = half // sites
    sums = len(LINK_SUMS)
    right, left = lax.rem(me + 1, n), lax.rem(me + n - 1, n)

    barrier = pltpu.get_barrier_semaphore()

    def greet(d, carry):
        pl.semaphore_signal(barrier, inc=1, device_id={"ta": lax.rem(me + d, n)})
        return carry

    lax.fori_loop(1, n, greet, 0)
    inputs = [
        pltpu.make_async_copy(hbm, vmem, input_sem.at[i])
        for i, (hbm, vmem) in enumerate(
            ((source_ref, field.at[0]), (prol_ref, prol_in), (inverse_ref, inverse_in))
        )
    ]
    inputs[0].start()
    inputs[1].start()
    for s in range(sites):
        pltpu.make_async_copy(links_ref.at[0, s], raw.at[s], link_sem.at[s]).start()
    inputs[2].start()

    lane_site = lax.broadcasted_iota(jnp.int32, (1, width), 1) // rhs

    def over_sites(x):
        shift = rhs
        while shift < width:
            x = x + pltpu.roll(x, shift, 1)
            shift *= 2
        return x

    row_site = lax.broadcasted_iota(jnp.int32, (half, width), 0) // ks
    diagonal = row_site == lax.broadcasted_iota(jnp.int32, (half, width), 1) // rhs

    def rows_of(s, count=rhs):
        return pl.ds(pl.multiple_of(s * count, count), count)

    def dot_parts(a, b):
        p = dot(a, b)
        rows = a.shape[0] // 2
        return p[:rows, :width] + p[:rows, width:] + p[rows:, :width]

    def restrict():
        hi = jnp.concatenate([parts[s, :rhs] for s in range(sites)], axis=0)
        lo = jnp.concatenate([parts[s, rhs:] for s in range(sites)], axis=0)
        full = fold(dot_rows(prol_parts, hi)) + dot_rows(prol_parts[:half], lo)
        full = jnp.where(diagonal, full, 0.0)
        return functools.reduce(jnp.add, [full[s * ks : (s + 1) * ks] for s in range(sites)])

    def products(pairs, rows=1):
        packed = []
        for at in range(0, rows * sites, sites):
            sums_over = []
            for a, b in pairs[at : at + sites]:
                p = a * b
                p = functools.reduce(jnp.add, [p[s * rhs : (s + 1) * rhs] for s in range(sites)])
                sums_over.append(
                    functools.reduce(
                        jnp.add, [p[:, c : c + width] for c in range(0, comps, width)]
                    )
                )
            blank = [jnp.zeros((rhs, width), F32)] * (sites - len(sums_over))
            packed.append(
                jnp.sum(jnp.concatenate(sums_over + blank, axis=0).T, axis=0, keepdims=True)
            )
        return packed[0] if rows == 1 else jnp.concatenate(packed, axis=0)

    def columns(values):
        blank = [jnp.zeros((1, width), F32)] * (-len(values) % 8)
        turned = jnp.concatenate(list(values) + blank, axis=0).T
        return [turned[:, i : i + 1] for i in range(len(values))]

    def send_site(r, f, s):
        for side, to in ((0, left), (1, right)):
            pltpu.make_async_remote_copy(
                src_ref=field.at[f, rows_of(s)],
                dst_ref=halo.at[r, side, rows_of(s)],
                send_sem=halo_send.at[r, side],
                recv_sem=halo_recv.at[r, side, s],
                device_id={"ta": to},
            ).start()

    def send_field(r, f):
        for s in range(sites):
            send_site(r, f, s)

    def near(k, src, dst):
        return [
            pltpu.make_async_remote_copy(
                src_ref=src,
                dst_ref=dst.at[side],
                send_sem=near_send.at[k, side],
                recv_sem=near_recv.at[k, side],
                device_id={"ta": to},
            )
            for side, to in ((0, left), (1, right))
        ]

    pending = []

    core, chips = lax.rem(me, 2), n // 2
    partner = me + 1 - 2 * core

    def gather_copy(k, blocks):
        return pltpu.make_async_remote_copy(
            src_ref=gather.at[k, core, blocks],
            dst_ref=gather.at[k, core, blocks],
            send_sem=gather_send.at[k],
            recv_sem=gather_recv.at[k],
            device_id={"ta": partner},
        )

    def share_copy(k):
        return pltpu.make_async_remote_copy(
            src_ref=gather.at[k, core],
            dst_ref=gather.at[k, core],
            send_sem=share_send.at[k],
            recv_sem=share_recv.at[k],
            device_id={"ta": partner},
        )

    def exchange_large(k, value):
        stage[k] = value
        gather[k, core, me // 2] = value

        def one(d, carry):
            pltpu.make_async_remote_copy(
                src_ref=stage.at[k],
                dst_ref=gather.at[k, core, me // 2],
                send_sem=gather_send.at[k],
                recv_sem=gather_recv.at[k],
                device_id={"ta": lax.rem(me + 2 * d, n)},
            ).start()
            return carry

        lax.fori_loop(1, chips, one, 0)

    def share_large(k):
        gather_copy(k, pl.ds(0, chips - 1)).wait_recv()
        share_copy(k).start()

    def exchange_small(k, value):
        small_stage[k] = value
        small[k, me] = value

        def one(d, carry):
            pltpu.make_async_remote_copy(
                src_ref=small_stage.at[k],
                dst_ref=small.at[k, me],
                send_sem=small_send.at[k],
                recv_sem=small_recv.at[k],
                device_id={"ta": lax.rem(me + d, n)},
            ).start()
            return carry

        lax.fori_loop(1, n, one, 0)
        pending.append(
            pltpu.make_async_remote_copy(
                src_ref=small.at[k, pl.ds(0, n - 1)],
                dst_ref=small.at[k, pl.ds(0, n - 1)],
                send_sem=small_send.at[k],
                recv_sem=small_recv.at[k],
                device_id={"ta": right},
            )
        )

    def apply_links(s, vectors, first, last):
        k = slice(first * comps, last * comps)
        return fold(dot(vectors, lcat[s, 0, k]) + dot(vectors, lcat[s, 1, k]))

    def across(s):
        return (s + sites // 2) % sites, s ^ 1

    def load_inner(f):
        for s in range(sites):
            parts[s] = stacked_parts(field[f, s * rhs : (s + 1) * rhs])

    def inner():
        for s in range(sites):
            y, z = across(s)
            vectors = jnp.concatenate([parts[s], parts[y], parts[z]], axis=1)
            acc[s * rhs : (s + 1) * rhs] = apply_links(s, vectors, 0, INNER_SUMS)

    def outer(r, f, to, of_field, of_links, send=None, keep=False):
        def site(s, carry):
            for side in range(2):
                pltpu.make_async_remote_copy(
                    src_ref=field.at[0, rows_of(s)],
                    dst_ref=halo.at[r, side, rows_of(s)],
                    send_sem=halo_send.at[r, side],
                    recv_sem=halo_recv.at[r, side, s],
                    device_id={"ta": left},
                ).wait_recv()
            vectors = jnp.concatenate(
                [stacked_parts(halo[r, side, rows_of(s)]) for side in range(2)], axis=1
            )
            links = acc[rows_of(s)] + apply_links(s, vectors, INNER_SUMS, sums)
            new = of_field * field[f, rows_of(s)] + of_links * links
            field[to, rows_of(s)] = new
            if send is not None:
                send_site(send, to, s)
            if keep:
                parts[s] = stacked_parts(new)
            return carry

        lax.fori_loop(0, sites, site, 0)

    def image_of(c):
        last = len(c) - 1
        inside = [(c[i] - c[i - 1]) / STEP for i in range(1, last + 1)]
        return [c[0] / STEP] + inside + [-c[last] / STEP]

    def factor_of(gram, c, d):
        gd = [
            functools.reduce(jnp.add, [gram(i, j) * d[j] for j in range(len(d))])
            for i in range(len(d))
        ]
        across = functools.reduce(jnp.add, [gd[i] * c[i] for i in range(len(c))])
        squared = functools.reduce(jnp.add, [gd[i] * d[i] for i in range(len(d))])
        return DAMPING * across / squared

    def advance(c, x, d, factor):
        x = [x[i] + factor * c[i] if i < len(c) else x[i] for i in range(SWEEPS)]
        return [c[i] - factor * d[i] if i < len(c) else -factor * d[i] for i in range(len(d))], x

    def sweeps(gram, count):
        c = [jnp.ones((1, width), F32)]
        x = [jnp.zeros((1, width), F32)] * SWEEPS
        for _ in range(count):
            d = image_of(c)
            c, x = advance(c, x, d, factor_of(gram, c, d))
        return c, x

    def combine(coefficients, fields):
        return functools.reduce(jnp.add, [a * field[f] for a, f in zip(coefficients, fields)])

    images[...] = jnp.zeros(images.shape, BF16)
    inputs[0].wait()
    pl.semaphore_wait(barrier, n - 1)
    send_field(0, 0)
    load_inner(0)
    inputs[1].wait()
    prol_copies = near(0, prol_in, prol_halo)
    prol_parts = stacked_parts(prol_in[...])

    def prepare(s, carry):
        pltpu.make_async_copy(links_ref.at[0, s], raw.at[s], link_sem.at[s]).wait()
        for at, members in enumerate(LINK_SUMS):
            hi, lo = two_parts(functools.reduce(jnp.add, [raw[s, m] for m in members]).T)
            lcat[s, 0, at * comps : (at + 1) * comps] = hi
            lcat[s, 1, at * comps : (at + 1) * comps] = lo
        return carry

    lax.fori_loop(0, sites, prepare, 0)
    for k in range(SWEEPS + 1):
        value = jnp.concatenate(
            [restrict(), products([(field[k], field[i]) for i in range(k + 1)])], axis=0
        )
        exchange_large(k, value)
        if k == SWEEPS:
            for copy in prol_copies:
                copy.start()
        inner()
        if k:
            share_large(k - 1)
        if k < SWEEPS:
            outer(k, k, k + 1, 1.0 - STEP, -STEP, k + 1 if k + 1 < SWEEPS else None, True)

    inputs[2].wait()
    inverse_parts = stacked_parts(inverse_in[...])

    def total_of(slots, k, at, rows):
        return jnp.sum(slots.at[k][:, at : at + rows, :], axis=0)

    def unpack(total, i):
        row = total[i // sites : i // sites + 1]
        return over_sites(jnp.where(lane_site == i % sites, row, 0.0))

    def solve_coarse(coefficients):
        def spread(chip, carry):
            for half_chip in range(2):
                r = functools.reduce(
                    jnp.add,
                    [a * gather[k, half_chip, chip, :ks] for k, a in enumerate(coefficients)],
                )
                for s in range(sites):
                    hi, lo = two_parts(jnp.where(lane_site == s, r, 0.0))
                    row = ((2 * chip + half_chip) * sites + s) * ks
                    at = pl.ds(pl.multiple_of(row, ks), ks)
                    rall[at, :width] = hi
                    rall[at, width:] = lo
            return carry

        lax.fori_loop(0, chips, spread, 0)
        return over_sites(dot_parts(inverse_parts, rall[...]))

    grams = {}

    def gram(i, j):
        return grams[max(i, j), min(i, j)]

    def read_grams(k):
        share_copy(k).wait_recv()
        total = functools.reduce(jnp.add, [total_of(gather, (k, c), ks, 1) for c in range(2)])
        grams.update({(k, i): unpack(total, i) for i in range(k + 1)})

    for k in range(SWEEPS):
        read_grams(k)
    c, x = sweeps(gram, SWEEPS - 1)
    d = image_of(c)
    before = solve_coarse(c)
    share_large(SWEEPS)
    read_grams(SWEEPS)
    factor = factor_of(gram, c, d)
    coarse = before - factor * solve_coarse(d)
    coarse_out[...] = functools.reduce(
        jnp.add,
        [jnp.where(lane_site == s, coarse[s * ks : (s + 1) * ks], 0.0) for s in range(sites)],
    )
    coarse_copies = near(1, coarse_out, coarse_halo)
    for copy in coarse_copies:
        copy.start()
    send_field(SWEEPS, SWEEPS)
    c, x = advance(c, x, d, factor)
    turned = columns(c + x)
    c, x = turned[: len(c)], turned[len(c) :]
    field[7] = combine(c, range(SWEEPS + 1))

    for copy in prol_copies:
        copy.wait_recv()
    for at, block in enumerate((prol_in, prol_halo.at[0], prol_halo.at[1])):
        for s in range(sites):
            prol_sites[at, s] = stacked_parts(block[s * ks : (s + 1) * ks])
    for s in range(sites):
        y, z = across(s)
        terms = ((0, 0, s), (1, 0, y), (2, 0, z), (3, 1, s), (4, 2, s))
        for m, at, site in terms:
            value = apply_links(s, prol_sites[at, site], m, m + 1)
            if m == 0:
                value = value + prol_in[s * ks : (s + 1) * ks]
            row = at * half + site * ks
            images[s, 0, row : row + ks], images[s, 1, row : row + ks] = two_parts(value)

    there = [coarse]
    for side in range(2):
        coarse_copies[side].wait_recv()
        compact = coarse_halo[side]
        there += [over_sites(jnp.where(lane_site == s, compact, 0.0)) for s in range(sites)]
    there.append(jnp.zeros((images.shape[2] - 3 * half, width), F32))
    coarse_vectors = stacked_parts(jnp.concatenate(there, axis=0).T[:rhs])
    for s in range(sites):
        new = fold(dot(coarse_vectors, images[s, 0]) + dot(coarse_vectors, images[s, 1]))
        field[6, s * rhs : (s + 1) * rhs] = new
        send_site(4, 6, s)
        parts[s] = stacked_parts(new)
    exchange_small(0, products([(field[6], field[7]), (field[6], field[6])], SMALL_ROWS))
    outer(SWEEPS, SWEEPS, SWEEPS + 1, 1.0 - STEP, -STEP)
    inner()
    field[8] = combine(c, range(1, SWEEPS + 2))
    field[9] = combine(x, range(SWEEPS))
    spread_hi, spread_lo = two_parts(jnp.where(diagonal, coarse, 0.0).T)
    field[5] = (
        dot(spread_hi, prol_parts[:half])
        + dot(spread_lo, prol_parts[:half])
        + dot(spread_hi, prol_parts[half:])
    )
    outer(4, 6, 14, 1.0 - STEP, -STEP)
    pending[-1].wait_recv()
    pair = total_of(small, 0, 0, SMALL_ROWS)
    g = columns([unpack(pair, 0) / unpack(pair, 1)])[0]

    for s in range(sites):
        at = slice(s * rhs, (s + 1) * rhs)
        new = field[8, at] - g[at] * field[14, at]
        field[11, at] = new
        send_site(5, 11, s)
        parts[s] = stacked_parts(new)
    field[10] = field[7] - g * field[6]
    field[9] = field[9] + g * field[5]
    inner()
    outer(5, 11, 12, 1.0 - STEP, -STEP, 6, True)
    early = [(i, j) for i in range(3) for j in range(i + 1)]
    late = [(3, j) for j in range(4)]
    exchange_small(1, products([(field[10 + i], field[10 + j]) for i, j in early], SMALL_ROWS))
    inner()
    outer(6, 12, 13, 1.0 - STEP, -STEP)
    exchange_small(2, products([(field[10 + i], field[10 + j]) for i, j in late], SMALL_ROWS))
    for r in range(halo.shape[0]):
        for side in range(2):
            pltpu.make_async_remote_copy(
                src_ref=field.at[0],
                dst_ref=halo.at[r, side],
                send_sem=halo_send.at[r, side],
                recv_sem=halo_recv.at[r, side, 0],
                device_id={"ta": left},
            ).wait_send()
    for k in range(SWEEPS + 1):
        gather_copy(k, pl.ds(0, chips - 1)).wait_send()
        share_copy(k).wait_send()
    for copy in pending[:-1] + prol_copies + coarse_copies:
        copy.wait_send()
    pending[-2].wait_recv()
    total = total_of(small, 1, 0, SMALL_ROWS)
    grams = {pair: unpack(total, early.index(pair)) for pair in early}
    c, x = sweeps(gram, SWEEPS - 1)
    d = image_of(c)
    pending[-1].wait_recv()
    total = total_of(small, 2, 0, SMALL_ROWS)
    grams.update({pair: unpack(total, late.index(pair)) for pair in late})
    c, x = advance(c, x, d, factor_of(gram, c, d))
    turned = columns(c + x)
    residual_ref[...] = combine(turned[: len(c)], range(10, 14))
    solution_ref[...] = field[9] + combine(turned[len(c) :], range(10, 13))
    pending[-1].wait_send()


def hand_over(*refs):
    for got, out in zip(refs[:2], refs[2:]):
        out[...] = got[...]


def local(source, links, prolongator, coarse_inverse):
    n = lax.axis_size("ta")
    shape = source.shape
    _, sites, rhs, comps = shape
    ks = prolongator.shape[2]
    width, half = sites * rhs, sites * ks
    sums = len(LINK_SUMS)
    vmem = pl.BlockSpec(memory_space=pltpu.VMEM)
    dma = pltpu.SemaphoreType.DMA
    fields = (jax.ShapeDtypeStruct((width, comps), F32),) * 2
    results = pl.pallas_call(
        functools.partial(kernel, n),
        out_shape=fields,
        in_specs=[pl.BlockSpec(memory_space=pl.ANY)] * 4,
        out_specs=(vmem, vmem),
        scratch_shapes=[
            pltpu.VMEM((half, comps), F32),
            pltpu.VMEM(coarse_inverse.shape, F32),
            pltpu.VMEM(links.shape[1:], F32),
            pltpu.VMEM((sites, 2, sums * comps, comps), BF16),
            pltpu.VMEM((15, width, comps), F32),
            pltpu.VMEM((sites, 2 * rhs, comps), BF16),
            pltpu.VMEM((width, comps), F32),
            pltpu.VMEM((7, 2, width, comps), F32),
            pltpu.VMEM((2, half, comps), F32),
            pltpu.VMEM((3, sites, 2 * ks, comps), BF16),
            pltpu.VMEM((sites, 2, 4 * half, comps), BF16),
            pltpu.VMEM((ks, width), F32),
            pltpu.VMEM((2, ks, width), F32),
            pltpu.VMEM((SWEEPS + 1, ks + 1, width), F32),
            pltpu.VMEM((SWEEPS + 1, 2, n // 2, ks + 1, width), F32),
            pltpu.VMEM((3, SMALL_ROWS, width), F32),
            pltpu.VMEM((3, n, SMALL_ROWS, width), F32),
            pltpu.VMEM((n * half, 2 * width), BF16),
            dma((3,)),
            dma((sites,)),
            dma((7, 2)),
            dma((7, 2, sites)),
            dma((2, 2)),
            dma((2, 2)),
            dma((SWEEPS + 1,)),
            dma((SWEEPS + 1,)),
            dma((SWEEPS + 1,)),
            dma((SWEEPS + 1,)),
            dma((3,)),
            dma((3,)),
        ],
        compiler_params=pltpu.CompilerParams(
            collective_id=0, has_side_effects=True, vmem_limit_bytes=60 * 1024 * 1024
        ),
    )(
        source.reshape(width, comps),
        links,
        prolongator.reshape(half, comps),
        coarse_inverse,
    )
    results = pl.pallas_call(
        hand_over, out_shape=fields, in_specs=[vmem, vmem], out_specs=(vmem, vmem)
    )(*results)
    return tuple(r.reshape(shape) for r in results)


def solution(mesh):
    return jax.shard_map(
        local,
        mesh=mesh,
        in_specs=(
            P(("groups", "ta"), None, None, None),
            P("ta", None, None, None, None),
            P("ta", None, None, None),
            P("ta", None),
        ),
        out_specs=(P(("groups", "ta"), None, None, None), P(("groups", "ta"), None, None, None)),
        check_vma=False,
    )
```

time: 55 us -> 52.2 us (0.949)
  Pallas kernels: 54.3 us -> 51.4 us
    pallas_call x2, Pallas kernels: 54.3 us -> 51.4 us  [the longest x1 49.7 us: local(): pl.pallas_call(functools.partial(kernel, n), out_shape=fields, in_specs=[...]
where the time goes in v3:
time: 52.2 us; the launch traced here: 52 us
  Pallas kernels  51.4 us (98%)
  between operations  0.64 us (1%)
    pallas_call x1, Pallas kernels, local(): pl.pallas_call(functools.partial(kernel, n), out_shape=fields, in_specs=[...  49.7 us
    pallas_call x1, Pallas kernels, local(): pl.pallas_call(hand_over, out_shape=fields, in_specs=[vmem, vmem], out_sp...  1.68 us

profile of v3, /device:TPU:0, one launch (start us, length us, event | category | flops | bytes accessed | tf_op | source)
XLA Modules:
  0.0 52.0 jit_solution(16906070744901482815)
XLA Ops:
  0.6 49.7 %shard_map.59 = (f32[128,256]{1,0:T(8,128)}, f32[128,256]{1,0:T(8,128)}) custom-call(f32[128,256]{1,0:T(8,128)} %bitcast.4, f32[1,4,9,256,256]{4,3,2,1,0:T(8,128)} %links_ref.1, f32[64,256]{1,0:T(8,128)} %bitcast.5, f32[64,1024]{1,0:T(8,128)} %inverse_ref.1), custom_call_target="tpu_custom_call" | custom-call | tf_op jit(solution)/shard_map/pallas_call | solution.py:518
  50.3 1.7 %shard_map.60 = (f32[128,256]{1,0:T(8,128)}, f32[128,256]{1,0:T(8,128)}) custom-call(f32[128,256]{1,0:T(8,128)} %get-tuple-element.6.refs_0_, f32[128,256]{1,0:T(8,128)} %get-tuple-element.7.refs_1_), custom_call_target="tpu_custom_call" | custom-call | tf_op jit(solution)/shard_map/pallas_call | solution.py:564

commit v4 on v3

--- a/solution.py
+++ b/solution.py
@@ -501,8 +501,11 @@
 
 
 def hand_over(*refs):
-    for got, out in zip(refs[:2], refs[2:]):
-        out[...] = got[...]
+    copies = [pltpu.make_async_copy(refs[i], refs[2 + i], refs[4].at[i]) for i in range(2)]
+    for copy in copies:
+        copy.start()
+    for copy in copies:
+        copy.wait()
 
 
 def local(source, links, prolongator, coarse_inverse):
@@ -517,7 +520,7 @@
     fields = (jax.ShapeDtypeStruct((width, comps), F32),) * 2
     results = pl.pallas_call(
         functools.partial(kernel, n),
-        out_shape=fields,
+        out_shape=(pltpu.VMEM((width, comps), F32),) * 2,
         in_specs=[pl.BlockSpec(memory_space=pl.ANY)] * 4,
         out_specs=(vmem, vmem),
         scratch_shapes=[
@@ -562,8 +565,10 @@
         coarse_inverse,
     )
     results = pl.pallas_call(
-        hand_over, out_shape=fields, in_specs=[vmem, vmem], out_specs=(vmem, vmem)
-    )(*results)
+        hand_over, out_shape=fields, in_specs=[vmem] * 2,
+        out_specs=(pl.BlockSpec(memory_space=pl.ANY),) * 2, scratch_shapes=[dma((2,))],
+        compiler_params=pltpu.CompilerParams(vmem_limit_bytes=1024 * 1024),
+    )(*[pltpu.with_memory_space_constraint(r, pltpu.VMEM) for r in results])
     return tuple(r.reshape(shape) for r in results)
 
 

time: 52.2 us -> 50.5 us (0.967)
  Pallas kernels: 51.4 us -> 49.7 us
    pallas_call x2, Pallas kernels: 51.4 us -> 49.7 us  [the longest x1 49 us: local(): pl.pallas_call(functools.partial(kernel, n), out_shape=(pltpu.VMEM((width...]
where the time goes in v4:
time: 50.5 us; the launch traced here: 50.4 us
  Pallas kernels  49.7 us (98%)
  between operations  0.64 us (1%)
    pallas_call x1, Pallas kernels, local(): pl.pallas_call(functools.partial(kernel, n), out_shape=(pltpu.VMEM((width...  49 us

profile of v4, /device:TPU:0, one launch (start us, length us, event | category | flops | bytes accessed | tf_op | source)
XLA Modules:
  0.0 50.4 jit_solution(11154259379933277983)
XLA Ops:
  0.6 49.0 %shard_map.59 = (f32[128,256]{1,0:T(8,128)S(1)}, f32[128,256]{1,0:T(8,128)S(1)}) custom-call(f32[128,256]{1,0:T(8,128)} %bitcast.4, f32[1,4,9,256,256]{4,3,2,1,0:T(8,128)} %links_ref.1, f32[64,256]{1,0:T(8,128)} %bitcast.5, f32[64,1024]{1,0:T(8,128)} %inverse_ref.1), custom_call_target="tpu_custom_call" | custom-call | tf_op jit(solution)/shard_map/pallas_call | solution.py:521
  49.6 0.7 %shard_map.60 = (f32[128,256]{1,0:T(8,128)}, f32[128,256]{1,0:T(8,128)}) custom-call(f32[128,256]{1,0:T(8,128)S(1)} %get-tuple-element.6.refs_0_, f32[128,256]{1,0:T(8,128)S(1)} %get-tuple-element.7.refs_1_), custom_call_target="tpu_custom_call" | custom-call | tf_op jit(solution)/shard_map/pallas_call | solution.py:567

commit v5 on v4

--- a/solution.py
+++ b/solution.py
@@ -60,6 +60,7 @@
     images,
     coarse_out,
     coarse_halo,
+    acc_coarse,
     stage,
     gather,
     small_stage,
@@ -86,6 +87,10 @@
     ks = half // sites
     sums = len(LINK_SUMS)
     right, left = lax.rem(me + 1, n), lax.rem(me + n - 1, n)
+    upper = me >= n // 2
+
+    def far_first(start, d):
+        return lax.rem(start + jnp.where(upper, d, n - d), n)
 
     barrier = pltpu.get_barrier_semaphore()
 
@@ -209,21 +214,29 @@
         stage[k] = value
         gather[k, core, me // 2] = value
 
-        def one(d, carry):
+        def send(to, send_sem, recv_sem):
             pltpu.make_async_remote_copy(
                 src_ref=stage.at[k],
                 dst_ref=gather.at[k, core, me // 2],
-                send_sem=gather_send.at[k],
-                recv_sem=gather_recv.at[k],
-                device_id={"ta": lax.rem(me + 2 * d, n)},
+                send_sem=send_sem.at[k],
+                recv_sem=recv_sem.at[k],
+                device_id={"ta": to},
             ).start()
+
+        def one(d, carry):
+            send(far_first(me, 2 * d), gather_send, gather_recv)
+            if k == SWEEPS:
+                send(far_first(partner, 2 * d), share_send, share_recv)
             return carry
 
         lax.fori_loop(1, chips, one, 0)
+        if k == SWEEPS:
+            send(partner, share_send, share_recv)
 
     def share_large(k):
         gather_copy(k, pl.ds(0, chips - 1)).wait_recv()
-        share_copy(k).start()
+        if k < SWEEPS:
+            share_copy(k).start()
 
     def exchange_small(k, value):
         small_stage[k] = value
@@ -235,7 +248,7 @@
                 dst_ref=small.at[k, me],
                 send_sem=small_send.at[k],
                 recv_sem=small_recv.at[k],
-                device_id={"ta": lax.rem(me + d, n)},
+                device_id={"ta": far_first(me, d)},
             ).start()
             return carry
 
@@ -261,8 +274,10 @@
         for s in range(sites):
             parts[s] = stacked_parts(field[f, s * rhs : (s + 1) * rhs])
 
-    def inner():
+    def inner(send=None):
         for s in range(sites):
+            if send is not None:
+                send_site(*send, s)
             y, z = across(s)
             vectors = jnp.concatenate([parts[s], parts[y], parts[z]], axis=1)
             acc[s * rhs : (s + 1) * rhs] = apply_links(s, vectors, 0, INNER_SUMS)
@@ -344,6 +359,7 @@
         )
         exchange_large(k, value)
         if k == SWEEPS:
+            send_field(k, k)
             for copy in prol_copies:
                 copy.start()
         inner()
@@ -377,7 +393,7 @@
                     rall[at, width:] = lo
             return carry
 
-        lax.fori_loop(0, chips, spread, 0)
+        lax.fori_loop(0, chips, spread, 0, unroll=4)
         return over_sites(dot_parts(inverse_parts, rall[...]))
 
     grams = {}
@@ -399,14 +415,10 @@
     read_grams(SWEEPS)
     factor = factor_of(gram, c, d)
     coarse = before - factor * solve_coarse(d)
-    coarse_out[...] = functools.reduce(
-        jnp.add,
-        [jnp.where(lane_site == s, coarse[s * ks : (s + 1) * ks], 0.0) for s in range(sites)],
-    )
+    coarse_out[...] = jnp.concatenate([coarse, jnp.zeros((width - half, width), F32)], axis=0).T[:rhs]
     coarse_copies = near(1, coarse_out, coarse_halo)
     for copy in coarse_copies:
         copy.start()
-    send_field(SWEEPS, SWEEPS)
     c, x = advance(c, x, d, factor)
     turned = columns(c + x)
     c, x = turned[: len(c)], turned[len(c) :]
@@ -427,15 +439,23 @@
             row = at * half + site * ks
             images[s, 0, row : row + ks], images[s, 1, row : row + ks] = two_parts(value)
 
-    there = [coarse]
-    for side in range(2):
-        coarse_copies[side].wait_recv()
-        compact = coarse_halo[side]
-        there += [over_sites(jnp.where(lane_site == s, compact, 0.0)) for s in range(sites)]
-    there.append(jnp.zeros((images.shape[2] - 3 * half, width), F32))
-    coarse_vectors = stacked_parts(jnp.concatenate(there, axis=0).T[:rhs])
+    def vectors_of(block):
+        return stacked_parts(block[:, :half])
+
+    def part_of(s, vectors, at):
+        k = slice(at * half, (at + 1) * half)
+        return fold(dot(vectors, images[s, 0, k]) + dot(vectors, images[s, 1, k]))
+
+    own = vectors_of(coarse_out[...])
     for s in range(sites):
-        new = fold(dot(coarse_vectors, images[s, 0]) + dot(coarse_vectors, images[s, 1]))
+        acc_coarse[s * rhs : (s + 1) * rhs] = part_of(s, own, 0)
+    for copy in coarse_copies:
+        copy.wait_recv()
+    around = jnp.concatenate([vectors_of(coarse_halo[side]) for side in range(2)], axis=1)
+    for s in range(sites):
+        k = slice(half, 3 * half)
+        links = fold(dot(around, images[s, 0, k]) + dot(around, images[s, 1, k]))
+        new = acc_coarse[s * rhs : (s + 1) * rhs] + links
         field[6, s * rhs : (s + 1) * rhs] = new
         send_site(4, 6, s)
         parts[s] = stacked_parts(new)
@@ -459,11 +479,10 @@
         at = slice(s * rhs, (s + 1) * rhs)
         new = field[8, at] - g[at] * field[14, at]
         field[11, at] = new
-        send_site(5, 11, s)
         parts[s] = stacked_parts(new)
+    inner((5, 11))
     field[10] = field[7] - g * field[6]
     field[9] = field[9] + g * field[5]
-    inner()
     outer(5, 11, 12, 1.0 - STEP, -STEP, 6, True)
     early = [(i, j) for i in range(3) for j in range(i + 1)]
     late = [(3, j) for j in range(4)]
@@ -535,8 +554,9 @@
             pltpu.VMEM((2, half, comps), F32),
             pltpu.VMEM((3, sites, 2 * ks, comps), BF16),
             pltpu.VMEM((sites, 2, 4 * half, comps), BF16),
-            pltpu.VMEM((ks, width), F32),
-            pltpu.VMEM((2, ks, width), F32),
+            pltpu.VMEM((rhs, width), F32),
+            pltpu.VMEM((2, rhs, width), F32),
+            pltpu.VMEM((width, comps), F32),
             pltpu.VMEM((SWEEPS + 1, ks + 1, width), F32),
             pltpu.VMEM((SWEEPS + 1, 2, n // 2, ks + 1, width), F32),
             pltpu.VMEM((3, SMALL_ROWS, width), F32),

time: 50.5 us -> 49.7 us (0.984)
  Pallas kernels: 49.7 us -> 48.9 us
    pallas_call x1, Pallas kernels: 49 us -> 48.2 us  [local(): pl.pallas_call(functools.partial(kernel, n), out_shape=(pltpu.VMEM((width...]
where the time goes in v5:
time: 49.7 us; the launch traced here: 49.6 us
  Pallas kernels  48.9 us (98%)
  between operations  0.64 us (1%)
    pallas_call x1, Pallas kernels, local(): pl.pallas_call(functools.partial(kernel, n), out_shape=(pltpu.VMEM((width...  48.2 us

profile of v5, /device:TPU:0, one launch (start us, length us, event | category | flops | bytes accessed | tf_op | source)
XLA Modules:
  0.0 49.6 jit_solution(6034358596551196188)
XLA Ops:
  0.6 48.2 %shard_map.59 = (f32[128,256]{1,0:T(8,128)S(1)}, f32[128,256]{1,0:T(8,128)S(1)}) custom-call(f32[128,256]{1,0:T(8,128)} %bitcast.4, f32[1,4,9,256,256]{4,3,2,1,0:T(8,128)} %links_ref.1, f32[64,256]{1,0:T(8,128)} %bitcast.5, f32[64,1024]{1,0:T(8,128)} %inverse_ref.1), custom_call_target="tpu_custom_call" | custom-call | tf_op jit(solution)/shard_map/pallas_call | solution.py:540
  48.9 0.7 %shard_map.60 = (f32[128,256]{1,0:T(8,128)}, f32[128,256]{1,0:T(8,128)}) custom-call(f32[128,256]{1,0:T(8,128)S(1)} %get-tuple-element.6.refs_0_, f32[128,256]{1,0:T(8,128)S(1)} %get-tuple-element.7.refs_1_), custom_call_target="tpu_custom_call" | custom-call | tf_op jit(solution)/shard_map/pallas_call | solution.py:587

commit v6 on v5

--- a/solution.py
+++ b/solution.py
@@ -70,6 +70,7 @@
     link_sem,
     halo_send,
     halo_recv,
+    late_recv,
     near_send,
     near_recv,
     gather_send,
@@ -161,13 +162,16 @@
         turned = jnp.concatenate(list(values) + blank, axis=0).T
         return [turned[:, i : i + 1] for i in range(len(values))]
 
+    def halo_arrival(r, side, s):
+        return late_recv.at[side] if r == SWEEPS else halo_recv.at[r % 2, side, s]
+
     def send_site(r, f, s):
         for side, to in ((0, left), (1, right)):
             pltpu.make_async_remote_copy(
                 src_ref=field.at[f, rows_of(s)],
                 dst_ref=halo.at[r, side, rows_of(s)],
-                send_sem=halo_send.at[r, side],
-                recv_sem=halo_recv.at[r, side, s],
+                send_sem=halo_send,
+                recv_sem=halo_arrival(r, side, s),
                 device_id={"ta": to},
             ).start()
 
@@ -180,8 +184,8 @@
             pltpu.make_async_remote_copy(
                 src_ref=src,
                 dst_ref=dst.at[side],
-                send_sem=near_send.at[k, side],
-                recv_sem=near_recv.at[k, side],
+                send_sem=near_send.at[k],
+                recv_sem=near_recv.at[k],
                 device_id={"ta": to},
             )
             for side, to in ((0, left), (1, right))
@@ -196,7 +200,7 @@
         return pltpu.make_async_remote_copy(
             src_ref=gather.at[k, core, blocks],
             dst_ref=gather.at[k, core, blocks],
-            send_sem=gather_send.at[k],
+            send_sem=gather_send,
             recv_sem=gather_recv.at[k],
             device_id={"ta": partner},
         )
@@ -205,7 +209,7 @@
         return pltpu.make_async_remote_copy(
             src_ref=gather.at[k, core],
             dst_ref=gather.at[k, core],
-            send_sem=share_send.at[k],
+            send_sem=share_send,
             recv_sem=share_recv.at[k],
             device_id={"ta": partner},
         )
@@ -218,7 +222,7 @@
             pltpu.make_async_remote_copy(
                 src_ref=stage.at[k],
                 dst_ref=gather.at[k, core, me // 2],
-                send_sem=send_sem.at[k],
+                send_sem=send_sem,
                 recv_sem=recv_sem.at[k],
                 device_id={"ta": to},
             ).start()
@@ -246,7 +250,7 @@
             pltpu.make_async_remote_copy(
                 src_ref=small_stage.at[k],
                 dst_ref=small.at[k, me],
-                send_sem=small_send.at[k],
+                send_sem=small_send,
                 recv_sem=small_recv.at[k],
                 device_id={"ta": far_first(me, d)},
             ).start()
@@ -257,7 +261,7 @@
             pltpu.make_async_remote_copy(
                 src_ref=small.at[k, pl.ds(0, n - 1)],
                 dst_ref=small.at[k, pl.ds(0, n - 1)],
-                send_sem=small_send.at[k],
+                send_sem=small_send,
                 recv_sem=small_recv.at[k],
                 device_id={"ta": right},
             )
@@ -283,15 +287,22 @@
             acc[s * rhs : (s + 1) * rhs] = apply_links(s, vectors, 0, INNER_SUMS)
 
     def outer(r, f, to, of_field, of_links, send=None, keep=False):
-        def site(s, carry):
+        def arrived(rows, s):
             for side in range(2):
                 pltpu.make_async_remote_copy(
-                    src_ref=field.at[0, rows_of(s)],
-                    dst_ref=halo.at[r, side, rows_of(s)],
-                    send_sem=halo_send.at[r, side],
-                    recv_sem=halo_recv.at[r, side, s],
+                    src_ref=field.at[0, rows],
+                    dst_ref=halo.at[r, side, rows],
+                    send_sem=halo_send,
+                    recv_sem=halo_arrival(r, side, s),
                     device_id={"ta": left},
                 ).wait_recv()
+
+        if r == SWEEPS:
+            arrived(slice(None), 0)
+
+        def site(s, carry):
+            if r != SWEEPS:
+                arrived(rows_of(s), s)
             vectors = jnp.concatenate(
                 [stacked_parts(halo[r, side, rows_of(s)]) for side in range(2)], axis=1
             )
@@ -424,8 +435,16 @@
     c, x = turned[: len(c)], turned[len(c) :]
     field[7] = combine(c, range(SWEEPS + 1))
 
-    for copy in prol_copies:
-        copy.wait_recv()
+    def both_arrived(k, dst):
+        pltpu.make_async_remote_copy(
+            src_ref=dst,
+            dst_ref=dst,
+            send_sem=near_send.at[k],
+            recv_sem=near_recv.at[k],
+            device_id={"ta": left},
+        ).wait_recv()
+
+    both_arrived(0, prol_halo)
     for at, block in enumerate((prol_in, prol_halo.at[0], prol_halo.at[1])):
         for s in range(sites):
             prol_sites[at, s] = stacked_parts(block[s * ks : (s + 1) * ks])
@@ -449,8 +468,7 @@
     own = vectors_of(coarse_out[...])
     for s in range(sites):
         acc_coarse[s * rhs : (s + 1) * rhs] = part_of(s, own, 0)
-    for copy in coarse_copies:
-        copy.wait_recv()
+    both_arrived(1, coarse_halo)
     around = jnp.concatenate([vectors_of(coarse_halo[side]) for side in range(2)], axis=1)
     for s in range(sites):
         k = slice(half, 3 * half)
@@ -490,20 +508,16 @@
     inner()
     outer(6, 12, 13, 1.0 - STEP, -STEP)
     exchange_small(2, products([(field[10 + i], field[10 + j]) for i, j in late], SMALL_ROWS))
-    for r in range(halo.shape[0]):
-        for side in range(2):
-            pltpu.make_async_remote_copy(
-                src_ref=field.at[0],
-                dst_ref=halo.at[r, side],
-                send_sem=halo_send.at[r, side],
-                recv_sem=halo_recv.at[r, side, 0],
-                device_id={"ta": left},
-            ).wait_send()
-    for k in range(SWEEPS + 1):
-        gather_copy(k, pl.ds(0, chips - 1)).wait_send()
-        share_copy(k).wait_send()
-    for copy in pending[:-1] + prol_copies + coarse_copies:
-        copy.wait_send()
+    def all_sent(ref, sem):
+        pltpu.make_async_remote_copy(
+            src_ref=ref, dst_ref=ref, send_sem=sem, recv_sem=late_recv.at[0], device_id={"ta": left}
+        ).wait_send()
+
+    all_sent(halo, halo_send)
+    all_sent(gather.at[:, 0, pl.ds(0, chips - 1)], gather_send)
+    all_sent(gather.at[:, 0], share_send)
+    all_sent(prol_halo, near_send.at[0])
+    all_sent(coarse_halo, near_send.at[1])
     pending[-2].wait_recv()
     total = total_of(small, 1, 0, SMALL_ROWS)
     grams = {pair: unpack(total, early.index(pair)) for pair in early}
@@ -516,7 +530,7 @@
     turned = columns(c + x)
     residual_ref[...] = combine(turned[: len(c)], range(10, 14))
     solution_ref[...] = field[9] + combine(turned[len(c) :], range(10, 13))
-    pending[-1].wait_send()
+    all_sent(small.at[:, pl.ds(0, n - 1)], small_send)
 
 
 def hand_over(*refs):
@@ -564,15 +578,16 @@
             pltpu.VMEM((n * half, 2 * width), BF16),
             dma((3,)),
             dma((sites,)),
-            dma((7, 2)),
-            dma((7, 2, sites)),
-            dma((2, 2)),
-            dma((2, 2)),
+            dma,
+            dma((2, 2, sites)),
+            dma((2,)),
+            dma((2,)),
+            dma((2,)),
+            dma,
             dma((SWEEPS + 1,)),
+            dma,
             dma((SWEEPS + 1,)),
-            dma((SWEEPS + 1,)),
-            dma((SWEEPS + 1,)),
-            dma((3,)),
+            dma,
             dma((3,)),
         ],
         compiler_params=pltpu.CompilerParams(

time: 49.7 us -> 49.2 us (0.990)
  Pallas kernels: 48.9 us -> 48.4 us
    pallas_call x1, Pallas kernels: 48.2 us -> 47.7 us  [local(): pl.pallas_call(functools.partial(kernel, n), out_shape=(pltpu.VMEM((width...]
where the time goes in v6:
time: 49.2 us; the launch traced here: 49 us
  Pallas kernels  48.4 us (98%)
  between operations  0.64 us (1%)
    pallas_call x1, Pallas kernels, local(): pl.pallas_call(functools.partial(kernel, n), out_shape=(pltpu.VMEM((width...  47.7 us

profile of v6, /device:TPU:0, one launch (start us, length us, event | category | flops | bytes accessed | tf_op | source)
XLA Modules:
  0.0 49.0 jit_solution(4682970077642878348)
XLA Ops:
  0.6 47.7 %shard_map.59 = (f32[128,256]{1,0:T(8,128)S(1)}, f32[128,256]{1,0:T(8,128)S(1)}) custom-call(f32[128,256]{1,0:T(8,128)} %bitcast.4, f32[1,4,9,256,256]{4,3,2,1,0:T(8,128)} %links_ref.1, f32[64,256]{1,0:T(8,128)} %bitcast.5, f32[64,1024]{1,0:T(8,128)} %inverse_ref.1), custom_call_target="tpu_custom_call" | custom-call | tf_op jit(solution)/shard_map/pallas_call | solution.py:554
  48.3 0.7 %shard_map.60 = (f32[128,256]{1,0:T(8,128)}, f32[128,256]{1,0:T(8,128)}) custom-call(f32[128,256]{1,0:T(8,128)S(1)} %get-tuple-element.6.refs_0_, f32[128,256]{1,0:T(8,128)S(1)} %get-tuple-element.7.refs_1_), custom_call_target="tpu_custom_call" | custom-call | tf_op jit(solution)/shard_map/pallas_call | solution.py:602

commit v7 on v6

--- a/solution.py
+++ b/solution.py
@@ -475,9 +475,12 @@
         links = fold(dot(around, images[s, 0, k]) + dot(around, images[s, 1, k]))
         new = acc_coarse[s * rhs : (s + 1) * rhs] + links
         field[6, s * rhs : (s + 1) * rhs] = new
+        if s < sites // 2:
+            send_site(4, 6, s)
+    exchange_small(0, products([(field[6], field[7]), (field[6], field[6])], SMALL_ROWS))
+    for s in range(sites // 2, sites):
         send_site(4, 6, s)
-        parts[s] = stacked_parts(new)
-    exchange_small(0, products([(field[6], field[7]), (field[6], field[6])], SMALL_ROWS))
+    load_inner(6)
     outer(SWEEPS, SWEEPS, SWEEPS + 1, 1.0 - STEP, -STEP)
     inner()
     field[8] = combine(c, range(1, SWEEPS + 2))

time: 49.2 us -> 49.1 us (level)
  no operation moved by 1% of the time
where the time goes in v7:
time: 49.1 us; the launch traced here: 48.9 us
  Pallas kernels  48.3 us (98%)
  between operations  0.64 us (1%)
    pallas_call x1, Pallas kernels, local(): pl.pallas_call(functools.partial(kernel, n), out_shape=(pltpu.VMEM((width...  47.6 us

profile of v7, /device:TPU:0, one launch (start us, length us, event | category | flops | bytes accessed | tf_op | source)
XLA Modules:
  0.0 48.9 jit_solution(7470146503527946769)
XLA Ops:
  0.6 47.6 %shard_map.59 = (f32[128,256]{1,0:T(8,128)S(1)}, f32[128,256]{1,0:T(8,128)S(1)}) custom-call(f32[128,256]{1,0:T(8,128)} %bitcast.4, f32[1,4,9,256,256]{4,3,2,1,0:T(8,128)} %links_ref.1, f32[64,256]{1,0:T(8,128)} %bitcast.5, f32[64,1024]{1,0:T(8,128)} %inverse_ref.1), custom_call_target="tpu_custom_call" | custom-call | tf_op jit(solution)/shard_map/pallas_call | solution.py:557
  48.2 0.7 %shard_map.60 = (f32[128,256]{1,0:T(8,128)}, f32[128,256]{1,0:T(8,128)}) custom-call(f32[128,256]{1,0:T(8,128)S(1)} %get-tuple-element.6.refs_0_, f32[128,256]{1,0:T(8,128)S(1)} %get-tuple-element.7.refs_1_), custom_call_target="tpu_custom_call" | custom-call | tf_op jit(solution)/shard_map/pallas_call | solution.py:605

commit v8 on v7

--- a/solution.py
+++ b/solution.py
@@ -162,8 +162,8 @@
         turned = jnp.concatenate(list(values) + blank, axis=0).T
         return [turned[:, i : i + 1] for i in range(len(values))]
 
-    def halo_arrival(r, side, s):
-        return late_recv.at[side] if r == SWEEPS else halo_recv.at[r % 2, side, s]
+    def halo_arrival(r, s):
+        return late_recv if r == SWEEPS else halo_recv.at[r % 2, s]
 
     def send_site(r, f, s):
         for side, to in ((0, left), (1, right)):
@@ -171,7 +171,7 @@
                 src_ref=field.at[f, rows_of(s)],
                 dst_ref=halo.at[r, side, rows_of(s)],
                 send_sem=halo_send,
-                recv_sem=halo_arrival(r, side, s),
+                recv_sem=halo_arrival(r, s),
                 device_id={"ta": to},
             ).start()
 
@@ -288,14 +288,13 @@
 
     def outer(r, f, to, of_field, of_links, send=None, keep=False):
         def arrived(rows, s):
-            for side in range(2):
-                pltpu.make_async_remote_copy(
-                    src_ref=field.at[0, rows],
-                    dst_ref=halo.at[r, side, rows],
-                    send_sem=halo_send,
-                    recv_sem=halo_arrival(r, side, s),
-                    device_id={"ta": left},
-                ).wait_recv()
+            pltpu.make_async_remote_copy(
+                src_ref=halo.at[r, :, rows],
+                dst_ref=halo.at[r, :, rows],
+                send_sem=halo_send,
+                recv_sem=halo_arrival(r, s),
+                device_id={"ta": left},
+            ).wait_recv()
 
         if r == SWEEPS:
             arrived(slice(None), 0)
@@ -513,7 +512,7 @@
     exchange_small(2, products([(field[10 + i], field[10 + j]) for i, j in late], SMALL_ROWS))
     def all_sent(ref, sem):
         pltpu.make_async_remote_copy(
-            src_ref=ref, dst_ref=ref, send_sem=sem, recv_sem=late_recv.at[0], device_id={"ta": left}
+            src_ref=ref, dst_ref=ref, send_sem=sem, recv_sem=late_recv, device_id={"ta": left}
         ).wait_send()
 
     all_sent(halo, halo_send)
@@ -582,8 +581,8 @@
             dma((3,)),
             dma((sites,)),
             dma,
-            dma((2, 2, sites)),
-            dma((2,)),
+            dma((2, sites)),
+            dma,
             dma((2,)),
             dma((2,)),
             dma,

time: 49.1 us -> 49 us (level)
  no operation moved by 1% of the time
where the time goes in v8:
time: 49 us; the launch traced here: 48.8 us
  Pallas kernels  48.2 us (98%)
  between operations  0.64 us (1%)
    pallas_call x1, Pallas kernels, local(): pl.pallas_call(functools.partial(kernel, n), out_shape=(pltpu.VMEM((width...  47.5 us

profile of v8, /device:TPU:0, one launch (start us, length us, event | category | flops | bytes accessed | tf_op | source)
XLA Modules:
  0.0 48.8 jit_solution(609149751914608339)
XLA Ops:
  0.6 47.5 %shard_map.59 = (f32[128,256]{1,0:T(8,128)S(1)}, f32[128,256]{1,0:T(8,128)S(1)}) custom-call(f32[128,256]{1,0:T(8,128)} %bitcast.4, f32[1,4,9,256,256]{4,3,2,1,0:T(8,128)} %links_ref.1, f32[64,256]{1,0:T(8,128)} %bitcast.5, f32[64,1024]{1,0:T(8,128)} %inverse_ref.1), custom_call_target="tpu_custom_call" | custom-call | tf_op jit(solution)/shard_map/pallas_call | solution.py:556
  48.1 0.7 %shard_map.60 = (f32[128,256]{1,0:T(8,128)}, f32[128,256]{1,0:T(8,128)}) custom-call(f32[128,256]{1,0:T(8,128)S(1)} %get-tuple-element.6.refs_0_, f32[128,256]{1,0:T(8,128)S(1)} %get-tuple-element.7.refs_1_), custom_call_target="tpu_custom_call" | custom-call | tf_op jit(solution)/shard_map/pallas_call | solution.py:604
